TPU v7x, 256 devices: a whole 4x4x8 slice. The times are simulated.
256 devices in a mesh: section: 16 (over y, x_hi, core), expert: 16 (over z, x_lo).
Axes of the slice: x: 4 (x_hi: 2, x_lo: 2; x = x_hi * 2 + x_lo), y: 4, z: 8, core: 2. Of those that a mesh axis runs over, the one named last changes fastest.
Arguments:
- grad_out: bfloat16 [16, 2048, 1024], P('section', 'expert'), may hold values from -6 to 6
- saved_inputs: bfloat16 [16, 2, 2048, 1024], P('section', None, 'expert'), may hold values from -6 to 6
- routes: int32 [16, 2, 2048, 8], P('section', None, 'expert'), may hold values from 0 to 31, all different within a row; in each aligned block of 128 rows (0 to 127, 128 to 255, ..., all dimensions but the last counted through in order) at most 40 rows name the same one
- gate_weights: float32 [16, 2, 2048, 8], P('section', None, 'expert'), may hold values from 0.05 to 0.3
- w_gate: bfloat16 [16, 32, 1024, 512], P('section', 'expert'), may hold values from -0.1875 to 0.1875
- w_up: bfloat16 [16, 32, 1024, 512], P('section', 'expert'), may hold values from -0.1875 to 0.1875
- w_down: bfloat16 [16, 32, 512, 1024], P('section', 'expert'), may hold values from -0.25 to 0.25
Outputs:
- input_grad: bfloat16 [16, 2048, 1024], P('section', 'expert')
Inputs may be any that keep to these rules, and one draw needn't show every extreme that they name: `routes`: each row names 8 different experts. In the rows of one device at one step (aligned blocks of 128 rows) no expert is named by more than 40 rows; in some blocks one expert is named by exactly 40.
All inputs are finite; a program needn't handle non-finite values.
Results may differ from a plain program's by a relative error of at most 0.007.
Values may be sent and summed in bfloat16 or wider, within the bound.
A program may use at most 64 MiB of HBM per device.

v0:
```python
import jax
import jax.numpy as jnp
from jax import lax
from jax.sharding import PartitionSpec as P

MOST = 40


def passed_along(value, axis, by):
    devices = lax.axis_size(axis)
    return lax.ppermute(value, axis, [(i, (i + by) % devices) for i in range(devices)])


def shards(grad_out, saved_inputs, routes, gate_weights, w_gate, w_up, w_down):
    owners = lax.axis_size("expert")
    gate_local = w_gate[0]
    up_local = w_up[0]
    down_local = w_down[0]
    local_count = gate_local.shape[0]
    expert_total = owners * local_count
    token_count = grad_out.shape[1]
    width = grad_out.shape[2]
    step_count = routes.shape[1]
    top_count = routes.shape[3]
    row_total = token_count * top_count

    def layout(step_index):
        flat_routes = routes[0, step_index].reshape(-1)
        one_hot = (
            flat_routes[:, None] == jnp.arange(expert_total, dtype=jnp.int32)[None, :]
        ).astype(jnp.int32)
        earlier = jnp.cumsum(one_hot, axis=0) - one_hot
        position = jnp.sum(earlier * one_hot, axis=1)
        slot_index = flat_routes * MOST + position
        token_index = jnp.arange(row_total, dtype=jnp.int32) // top_count
        slot_token = jnp.zeros((expert_total * MOST,), jnp.int32).at[slot_index].set(token_index)
        slot_live = jnp.zeros((expert_total * MOST,), jnp.int32).at[slot_index].set(1)
        return (slot_index, slot_token, slot_live)

    def pack(source, slot_token, slot_live):
        picked = jnp.where(slot_live[:, None] == 1, source[slot_token], jnp.zeros((), source.dtype))
        return picked.reshape(owners, local_count, MOST, width)

    plans = [layout(step_index) for step_index in range(step_count)]
    grad = grad_out[0]
    total = grad
    for step_index in range(step_count):
        slot_index, slot_token, slot_live = plans[step_index]
        grad_rows = pack(grad, slot_token, slot_live)
        input_rows = pack(saved_inputs[0, step_index], slot_token, slot_live)
        expert_input_rows = lax.all_to_all(
            input_rows, "expert", split_axis=0, concat_axis=0, tiled=True
        )
        expert_grad_rows = lax.all_to_all(
            grad_rows, "expert", split_axis=0, concat_axis=0, tiled=True
        )
        gate_pre = jnp.einsum(
            "sjmd,jdh->sjmh", expert_input_rows, gate_local, preferred_element_type=jnp.float32
        )
        up_pre = jnp.einsum(
            "sjmd,jdh->sjmh", expert_input_rows, up_local, preferred_element_type=jnp.float32
        )
        hidden_grad = jnp.einsum(
            "sjmd,jhd->sjmh", expert_grad_rows, down_local, preferred_element_type=jnp.float32
        )
        sigmoid_gate = jax.nn.sigmoid(gate_pre)
        gate_grad = (
            hidden_grad * up_pre * sigmoid_gate * (1.0 + gate_pre * (1.0 - sigmoid_gate))
        ).astype(jnp.bfloat16)
        up_grad = (hidden_grad * gate_pre * sigmoid_gate).astype(jnp.bfloat16)
        row_grad = jnp.einsum(
            "sjmh,jdh->sjmd", gate_grad, gate_local, preferred_element_type=jnp.float32
        )
        row_grad = row_grad + jnp.einsum(
            "sjmh,jdh->sjmd", up_grad, up_local, preferred_element_type=jnp.float32
        )
        row_grad = row_grad.astype(jnp.bfloat16)
        back_rows = lax.all_to_all(row_grad, "expert", split_axis=0, concat_axis=0, tiled=True)
        gathered = back_rows.reshape(expert_total * MOST, width)[slot_index].reshape(
            token_count, top_count, width
        )
        weights = gate_weights[0, step_index]
        summed = grad.astype(jnp.float32) + jnp.sum(
            weights[:, :, None] * gathered.astype(jnp.float32), axis=1
        )
        total = summed.astype(jnp.bfloat16)
        if step_index + 1 < step_count:
            grad = passed_along(total, "section", -1)
    return total[None]


def solution(mesh):
    placed = (
        P("section", "expert", None),
        P("section", None, "expert", None),
        P("section", None, "expert", None),
        P("section", None, "expert", None),
        P("section", "expert", None, None),
        P("section", "expert", None, None),
        P("section", "expert", None, None),
    )
    return jax.shard_map(
        shards, mesh=mesh, in_specs=placed, out_specs=P("section", "expert", None), check_vma=False
    )
```

profile of v0, /device:TPU:1, one launch (start us, length us, event | category | flops | bytes accessed | tf_op | source)
XLA Modules:
  0.0 512.7 jit_solution(9720386422153351338)
XLA Ops:
  0.0 0.9 fusion.92
  0.9 0.1 copy.32
  1.2 9.0 %reduce-window.14 = s32[32,8,128]{2,1,0:T(8,128)S(1)} reduce-window(s32[32,8,128]{2,1,0:T(8,128)S(1)} %fusion.75, s32[]{:T(128)} %constant.32.clone.1), window={size=1x1x128 pad=0_0x0_0x127_0}, to_apply=%region_0.0 | reduce-window | flops 4161536 | bytes 262148 | tf_op jit(solution)/shard_map/reduce-window
  10.3 0.1 copy.34
  10.5 0.1 broadcast_add_fusion.1
  10.6 0.1 copy.31
  10.9 4.3 scatter_custom_fusion.1
  15.3 1.1 slice_bitcast_fusion.1
  16.3 5.1 gather_fusion.1
  21.4 5.1 gather_fusion
  26.5 4.3 scatter_custom_fusion
  31.0 3.8 broadcast_select_fusion.3
  34.8 70.5 %all_to_all.30 = bf16[16,2,40,1024]{3,2,1,0:T(8,128)(2,1)} all-to-all(bf16[16,2,40,1024]{3,2,1,0:T(8,128)(2,1)S(1)} %get-tuple-element.12), channel_id=1, replica_groups=mesh['section'=16,'expert'=16] {'expert'}, dimensions={0} | all-to-all | bytes 5242880 | tf_op jit(solution)/shard_map/all_to_all | solution.py:51
  105.3 4.9 all-to-all-start
  110.2 5.5 %fusion.30 = f32[2,16,40,512]{3,2,1,0:T(8,128)} fusion(bf16[16,2,40,1024]{3,2,1,0:T(8,128)(2,1)} %all_to_all.30, bf16[1,2,1024,512]{3,2,1,0:T(8,128)(2,1)} %param.11), kind=kOutput, calls=%fused_computation.56 | convolution fusion | flops 1342177280 | bytes 7340032 | tf_op jit(solution)/shard_map/sjmd,jdh->sjmh/dot_general | solution.py:57
  115.7 54.2 %all-to-all-done = bf16[16,2,40,1024]{3,2,1,0:T(8,128)(2,1)} async-done(((bf16[16,2,40,1024]{3,2,1,0:T(8,128)(2,1)}), bf16[16,2,40,1024]{3,2,1,0:T(8,128)(2,1)}, u32[]{:S(2)}, u32[]{:S(2)}) %all-to-all-start) | async-done | bytes 2621472 | tf_op jit(solution)/shard_map/all_to_all | solution.py:54
  169.9 5.5 %fusion.24 = f32[2,16,40,512]{3,2,1,0:T(8,128)} fusion(bf16[16,2,40,1024]{3,2,1,0:T(8,128)(2,1)} %all-to-all-done, bf16[1,2,512,1024]{3,2,1,0:T(8,128)(2,1)} %param.13), kind=kOutput, calls=%fused_computation.46 | convolution fusion | flops 1342177280 | bytes 7340032 | tf_op jit(solution)/shard_map/sjmd,jhd->sjmh/dot_general | solution.py:63
  175.4 9.6 %fusion.37 = f32[2,16,40,1024]{3,2,1,0:T(8,128)} fusion(bf16[1,2,1024,512]{3,2,1,0:T(8,128)(2,1)} %param.11, f32[2,16,40,512]{3,2,1,0:T(8,128)} %fusion.30, f32[2,16,40,512]{3,2,1,0:T(8,128)} %fusion.24, bf16[16,2,40,1024]{3,2,1,0:T(8,128)(2,1)} %all_to_all.30, bf16[1,2,1024,512]{3,2,1,0:T(8,128)(2,1)S(1)} %copy-done), kind=kOutput, calls=%fused_computation.63 | convolution fusion | flops 2690908160 | bytes 17301504 | tf_op jit(solution)/shard_map/sjmh,jdh->sjmd/dot_general | solution.py:71
  185.0 5.7 %fusion.2 = bf16[16,2,40,1024]{3,2,0,1:T(8,128)(2,1)S(1)} fusion(f32[2,16,40,1024]{3,2,1,0:T(8,128)} %fusion.37, bf16[1,2,1024,512]{3,2,1,0:T(8,128)(2,1)S(1)} %copy-done, f32[2,16,40,512]{3,2,1,0:T(8,128)} %fusion.30, f32[2,16,40,512]{3,2,1,0:T(8,128)} %fusion.24), kind=kOutput, calls=%fused_computation.16 | convolution fusion | flops 1348730880 | bytes 15204352 | tf_op jit(solution)/shard_map/sjmh,jdh->sjmd/dot_general | solution.py:74
  190.7 1.9 copy.39
  192.5 5.9 %all-to-all-start.2 = ((bf16[16,2,40,1024]{3,2,1,0:T(8,128)(2,1)}), bf16[16,2,40,1024]{3,2,1,0:T(8,128)(2,1)}, u32[]{:S(2)}, u32[]{:S(2)}) async-start(bf16[16,2,40,1024]{3,2,1,0:T(8,128)(2,1)} %copy.39), calls=%async_computation.2 | async-start | bytes 5242880 | tf_op jit(solution)/shard_map/all_to_all | solution.py:78
  198.4 0.1 copy.42
  198.7 9.0 %reduce-window.16 = s32[32,8,128]{2,1,0:T(8,128)S(1)} reduce-window(s32[32,8,128]{2,1,0:T(8,128)S(1)} %fusion.76, s32[]{:T(128)} %constant.32.clone.1), window={size=1x1x128 pad=0_0x0_0x127_0}, to_apply=%region_6.7 | reduce-window | flops 4161536 | bytes 262148 | tf_op jit(solution)/shard_map/reduce-window.2
  207.8 0.1 copy.44
  208.2 0.1 mul.103
  208.5 4.3 scatter_custom_fusion.3
  212.8 4.5 scatter_custom_fusion.2
  217.6 40.8 %all-to-all-done.2 = bf16[16,2,40,1024]{3,2,1,0:T(8,128)(2,1)} async-done(((bf16[16,2,40,1024]{3,2,1,0:T(8,128)(2,1)}), bf16[16,2,40,1024]{3,2,1,0:T(8,128)(2,1)}, u32[]{:S(2)}, u32[]{:S(2)}) %all-to-all-start.2) | async-done | bytes 2621472 | tf_op jit(solution)/shard_map/all_to_all | solution.py:78
  258.4 8.1 %gather_fusion.2 = bf16[1024,1024]{1,0:T(8,128)(2,1)} fusion(bf16[1280,1024]{1,0:T(8,128)(2,1)} %bitcast.23, s32[1024]{0:T(1024)S(1)} %broadcast_clamp_fusion.1), kind=kCustom, calls=%fused_computation.2 | custom fusion | bytes 4198400 | tf_op jit(solution)/shard_map/gather | solution.py:79
  266.5 2.9 fusion.1
  269.5 2.5 collective-permute-start
  272.1 5.1 gather_fusion.4
  277.1 1.3 collective-permute-done
  278.4 5.1 gather_fusion.3
  283.6 3.8 broadcast_select_fusion.1
  287.4 61.8 %all_to_all.31 = bf16[16,2,40,1024]{3,2,1,0:T(8,128)(2,1)} all-to-all(bf16[16,2,40,1024]{3,2,1,0:T(8,128)(2,1)S(1)} %get-tuple-element.9), channel_id=1, replica_groups=mesh['section'=16,'expert'=16] {'expert'}, dimensions={0} | all-to-all | bytes 5242880 | tf_op jit(solution)/shard_map/all_to_all | solution.py:54
  349.2 4.5 all-to-all-start.4
  353.7 5.5 %fusion.22 = f32[2,16,40,512]{3,2,1,0:T(8,128)} fusion(bf16[16,2,40,1024]{3,2,1,0:T(8,128)(2,1)} %all_to_all.31, bf16[1,2,512,1024]{3,2,1,0:T(8,128)(2,1)} %param.13), kind=kOutput, calls=%fused_computation.44 | convolution fusion | flops 1342177280 | bytes 7340032 | tf_op jit(solution)/shard_map/sjmd,jhd->sjmh/dot_general | solution.py:63
  359.2 53.0 %all-to-all-done.4 = bf16[16,2,40,1024]{3,2,1,0:T(8,128)(2,1)} async-done(((bf16[16,2,40,1024]{3,2,1,0:T(8,128)(2,1)}), bf16[16,2,40,1024]{3,2,1,0:T(8,128)(2,1)}, u32[]{:S(2)}, u32[]{:S(2)}) %all-to-all-start.4) | async-done | bytes 2621472 | tf_op jit(solution)/shard_map/all_to_all | solution.py:51
  412.2 5.5 %fusion.26 = f32[2,16,40,512]{3,2,1,0:T(8,128)} fusion(bf16[16,2,40,1024]{3,2,1,0:T(8,128)(2,1)} %all-to-all-done.4, bf16[1,2,1024,512]{3,2,1,0:T(8,128)(2,1)} %param.11), kind=kOutput, calls=%fused_computation.52 | convolution fusion | flops 1342177280 | bytes 7340032 | tf_op jit(solution)/shard_map/sjmd,jdh->sjmh/dot_general | solution.py:57
  417.7 9.6 %fusion.34 = f32[2,16,40,1024]{3,2,1,0:T(8,128)} fusion(bf16[1,2,1024,512]{3,2,1,0:T(8,128)(2,1)} %param.11, f32[2,16,40,512]{3,2,1,0:T(8,128)} %fusion.26, f32[2,16,40,512]{3,2,1,0:T(8,128)} %fusion.22, bf16[16,2,40,1024]{3,2,1,0:T(8,128)(2,1)} %all-to-all-done.4, bf16[1,2,1024,512]{3,2,1,0:T(8,128)(2,1)S(1)} %copy-done), kind=kOutput, calls=%fused_computation.60 | convolution fusion | flops 2690908160 | bytes 17301504 | tf_op jit(solution)/shard_map/sjmh,jdh->sjmd/dot_general | solution.py:71
  427.3 5.7 %fusion.3 = bf16[16,2,40,1024]{3,2,0,1:T(8,128)(2,1)S(1)} fusion(f32[2,16,40,1024]{3,2,1,0:T(8,128)} %fusion.34, bf16[1,2,1024,512]{3,2,1,0:T(8,128)(2,1)S(1)} %copy-done, f32[2,16,40,512]{3,2,1,0:T(8,128)} %fusion.26, f32[2,16,40,512]{3,2,1,0:T(8,128)} %fusion.22), kind=kOutput, calls=%fused_computation.17 | convolution fusion | flops 1348730880 | bytes 15204352 | tf_op jit(solution)/shard_map/sjmh,jdh->sjmd/dot_general | solution.py:74
  433.0 1.9 copy.49
  434.9 6.3 %all-to-all-start.5 = ((bf16[16,2,40,1024]{3,2,1,0:T(8,128)(2,1)}), bf16[16,2,40,1024]{3,2,1,0:T(8,128)(2,1)}, u32[]{:S(2)}, u32[]{:S(2)}) async-start(bf16[16,2,40,1024]{3,2,1,0:T(8,128)(2,1)} %copy.49), calls=%async_computation.5 | async-start | bytes 5242880 | tf_op jit(solution)/shard_map/all_to_all | solution.py:78
  441.3 59.6 %all-to-all-done.5 = bf16[16,2,40,1024]{3,2,1,0:T(8,128)(2,1)} async-done(((bf16[16,2,40,1024]{3,2,1,0:T(8,128)(2,1)}), bf16[16,2,40,1024]{3,2,1,0:T(8,128)(2,1)}, u32[]{:S(2)}, u32[]{:S(2)}) %all-to-all-start.5) | async-done | bytes 2621472 | tf_op jit(solution)/shard_map/all_to_all | solution.py:78
  500.9 8.1 %gather_fusion.5 = bf16[1024,1024]{1,0:T(8,128)(2,1)} fusion(bf16[1280,1024]{1,0:T(8,128)(2,1)} %bitcast.39, s32[1024]{0:T(1024)S(1)} %broadcast_clamp_fusion), kind=kCustom, calls=%fused_computation.5 | custom fusion | bytes 4198400 | tf_op jit(solution)/shard_map/gather | solution.py:79
  509.0 2.9 fusion
  512.0 0.8 fusion.68
  (43 shorter events, 1.7 us)
Async XLA Ops:
  0.0 175.4 %copy-start = (bf16[1,2,1024,512]{3,2,1,0:T(8,128)(2,1)S(1)}, bf16[1,2,1024,512]{3,2,1,0:T(8,128)(2,1)}, u32[]{:S(2)}) copy-start(bf16[1,2,1024,512]{3,2,1,0:T(8,128)(2,1)} %param.12) | copy-start | bytes 6291460
  16.3 5.1 copy-start.1
  105.3 64.6 %all-to-all-start = ((bf16[16,2,40,1024]{3,2,1,0:T(8,128)(2,1)}), bf16[16,2,40,1024]{3,2,1,0:T(8,128)(2,1)}, u32[]{:S(2)}, u32[]{:S(2)}) async-start(bf16[16,2,40,1024]{3,2,1,0:T(8,128)(2,1)} %get-tuple-element.11), calls=%async_computation | async-start | bytes 5242880 | tf_op jit(solution)/shard_map/all_to_all | solution.py:54
  192.5 24.8 %copy-start.2 = (f32[1,2,128,8]{2,3,1,0:T(8,128)S(1)}, f32[1,2,128,8]{2,3,1,0:T(8,128)}, u32[]{:S(2)}) copy-start(f32[1,2,128,8]{2,3,1,0:T(8,128)} %param.10) | copy-start | bytes 24580
  192.5 65.9 %all-to-all-start.2 = ((bf16[16,2,40,1024]{3,2,1,0:T(8,128)(2,1)}), bf16[16,2,40,1024]{3,2,1,0:T(8,128)(2,1)}, u32[]{:S(2)}, u32[]{:S(2)}) async-start(bf16[16,2,40,1024]{3,2,1,0:T(8,128)(2,1)} %copy.39), calls=%async_computation.2 | async-start | bytes 5242880 | tf_op jit(solution)/shard_map/all_to_all | solution.py:78
  269.5 8.9 %collective-permute-start = (bf16[128,1024]{1,0:T(8,128)(2,1)S(1)}, bf16[128,1024]{1,0:T(8,128)(2,1)S(1)}, u32[]{:S(2)}, u32[]{:S(2)}) collective-permute-start(bf16[128,1024]{1,0:T(8,128)(2,1)S(1)} %add_convert_fusion.3), channel_id=1, source_target_pairs={{0,240},{16,0},{32,16},{48,32},{64,48},{80,64},{96,80},{112,96},{1... | collective-permute-start | bytes 786440 | tf_op jit(solution)/shard_map/ppermute | solution.py:11
  349.2 63.1 %all-to-all-start.4 = ((bf16[16,2,40,1024]{3,2,1,0:T(8,128)(2,1)}), bf16[16,2,40,1024]{3,2,1,0:T(8,128)(2,1)}, u32[]{:S(2)}, u32[]{:S(2)}) async-start(bf16[16,2,40,1024]{3,2,1,0:T(8,128)(2,1)} %get-tuple-element.10), calls=%async_computation.4 | async-start | bytes 5242880 | tf_op jit(solution)/shard_map/all_to_all | solution.py:51
  434.9 66.1 %all-to-all-start.5 = ((bf16[16,2,40,1024]{3,2,1,0:T(8,128)(2,1)}), bf16[16,2,40,1024]{3,2,1,0:T(8,128)(2,1)}, u32[]{:S(2)}, u32[]{:S(2)}) async-start(bf16[16,2,40,1024]{3,2,1,0:T(8,128)(2,1)} %copy.49), calls=%async_computation.5 | async-start | bytes 5242880 | tf_op jit(solution)/shard_map/all_to_all | solution.py:78
where the time goes:
time: 521 us; the launch traced here: 513 us
  waiting for transfers between devices  209 us (40%)
  blocking collectives  132 us (25%)
  local copies, waits for them, and re-layouts  60.9 us (12%)
  matrix products  52.5 us (10%)
  other arithmetic  33.7 us (6%)
  starting transfers between devices  24.1 us (5%)
    all_to_all x2, waiting for transfers between devices, shards(): lax.all_to_all(row_grad, 'expert', split_axis=0, concat_axis=0, tiled=True)  100 us
    all_to_all x1, blocking collectives, shards(): lax.all_to_all(input_rows, 'expert', split_axis=0, concat_axis=0, tiled=T...  70.5 us
    all_to_all x1, blocking collectives, shards(): lax.all_to_all(grad_rows, 'expert', split_axis=0, concat_axis=0, tiled=True)  61.8 us
    all_to_all x1, waiting for transfers between devices, shards(): lax.all_to_all(grad_rows, 'expert', split_axis=0, concat_axis=0, tiled=True)  54.2 us
    all_to_all x1, waiting for transfers between devices, shards(): lax.all_to_all(input_rows, 'expert', split_axis=0, concat_axis=0, tiled=T...  53 us
    gather x4, local copies, waits for them, and re-layouts, pack(): source[slot_token]  20.4 us
    dot_general x2, matrix products, shards(): jnp.einsum('sjmh,jdh->sjmd', gate_grad, gate_local, preferred_element_typ...  19.3 us
    another operation x6, other arithmetic  18.3 us
  transfers between devices with their start and end apart: 5, of which 5 were waited for; matrix products, arithmetic and copies ran while one was open for 7% of the time, Pallas kernels for 0%

commit v1 on v0

v1 whole, which is shorter than its diff:
```python
import jax
import jax.numpy as jnp
from jax import lax
from jax.experimental import pallas as pl
from jax.experimental.pallas import tpu as pltpu
from jax.sharding import PartitionSpec as P

BF = jnp.bfloat16
F32 = jnp.float32
TOK = 128
D = 1024
H = 512
CAP = 80
RING = 8
PLACE = {0: 0, 1: 1, 7: 2, 2: 3, 6: 4, 3: 5, 5: 6, 4: 7}
SEMS = 224


def nt(a, b):
    return lax.dot_general(a, b, (((1,), (1,)), ((), ())), preferred_element_type=F32)


def nn(a, b):
    return lax.dot_general(a, b, (((1,), (0,)), ((), ())), preferred_element_type=F32)


def kernel(
    grad_in, saved_in, table_in, wg_in, wu_in, wd_in, out_ref,
    g0, x0, x1, g1, tab, wg, wu, wd, part, l_core, l_down, l_up, tot, fin,
    xg, gg, gp, up, rw, ws, pos, post, ssem, rsem, lsem,
):
    s = lax.axis_index("section")
    e = lax.axis_index("expert")
    core = lax.rem(s, 2)
    x_lo = lax.rem(e, 2)
    mixed = core != x_lo
    other_core = s + 1 - 2 * core
    other_x = e + 1 - 2 * x_lo
    z_up = (s, lax.rem(e + 2, 16))
    z_down = (s, lax.rem(e + 14, 16))
    mate = (other_core, e)
    swap = (other_core, other_x)
    pass_to = (lax.rem(s + 16 - 2 * (1 - x_lo), 16), other_x)
    pass_from = (lax.rem(s + 2 * x_lo, 16), other_x)
    home = lax.select(mixed, other_x, e)

    barrier = pltpu.get_barrier_semaphore()
    for peer in (z_up, z_down, mate, swap, pass_to, pass_from):
        pl.semaphore_signal(barrier, inc=1, device_id=peer, device_id_type=pl.DeviceIdType.MESH)

    count = [0]
    sent = {}

    def make(src, dst, peer):
        i = count[0]
        count[0] += 1
        return pltpu.make_async_remote_copy(
            src_ref=src, dst_ref=dst, send_sem=ssem.at[i], recv_sem=rsem.at[i],
            device_id=peer, device_id_type=pl.DeviceIdType.MESH,
        )

    def send(key, src, dst, peer):
        copy = make(src, dst, peer)
        copy.start()
        sent[key] = copy

    moves = {}

    def enter(key, src, dst):
        i = len(moves)
        moves[key] = (pltpu.make_async_copy(src, dst, lsem.at[i]), make(src, dst, swap))

        @pl.when(jnp.logical_not(mixed))
        def _():
            moves[key][0].start()

        @pl.when(mixed)
        def _():
            moves[key][1].start()

    def entered(key):
        @pl.when(jnp.logical_not(mixed))
        def _():
            moves[key][0].wait()

        @pl.when(mixed)
        def _():
            moves[key][1].wait_recv()

    pl.semaphore_wait(barrier, 6)
    enter("t", table_in, tab.at[0, 0])
    enter("x0", saved_in.at[0], x0.at[0, 0])
    enter("g0", grad_in, g0.at[0, 0])
    for j in range(2):
        enter(("wg", j), wg_in.at[j], wg.at[j])
        enter(("wu", j), wu_in.at[j], wu.at[j])
        enter(("wd", j), wd_in.at[j], wd.at[j])
        if j == 0:
            enter("x1", saved_in.at[1], x1.at[0, 0])

    def rows(ch):
        return pl.ds(64 * ch, 64)

    def to_mate(name, buf, d, ch):
        k = PLACE[d]
        send((name, "c", d, ch), buf.at[k, 0, rows(ch)], buf.at[k, 1, rows(ch)], mate)

    def hop(name, buf, way, d, ch):
        src, dst = (d, d + 1) if way == "u" else ((8 - d) % 8, 7 - d)
        send(
            (name, way, d, ch), buf.at[PLACE[src], 0, rows(ch)], buf.at[PLACE[dst], 0, rows(ch)],
            z_up if way == "u" else z_down,
        )

    def gather_first(name, buf, ch):
        hop(name, buf, "u", 0, ch)
        hop(name, buf, "d", 0, ch)
        to_mate(name, buf, 0, ch)

    def gather_step(names, d):
        for ch in range(2):
            for name, buf in names:
                for way in "ud":
                    here = d if way == "u" else 8 - d
                    if d < 4 or (way == "u") == (ch == 0):
                        sent[name, way, d - 1, ch].wait_recv()
                        if d < 3 or (d == 3 and (way == "u") == (ch == 0)):
                            hop(name, buf, way, d, ch)
                        to_mate(name, buf, here, ch)

    def gathered(name, d):
        for ch in range(2):
            sent[name, "c", d, ch].wait_recv()

    def table_step(d):
        if d == 0:
            send(("t", "u", 0), tab.at[0, 0], tab.at[PLACE[1], 0], z_up)
            send(("t", "d", 0), tab.at[0, 0], tab.at[PLACE[7], 0], z_down)
            send(("t", "c", 0), tab.at[0, 0], tab.at[0, 1], mate)
            return
        sent["t", "u", d - 1].wait_recv()
        k = PLACE[d]
        if d < 4:
            send(("t", "u", d), tab.at[k, 0], tab.at[PLACE[d + 1], 0], z_up)
        send(("t", "c", d), tab.at[k, 0], tab.at[k, 1], mate)
        if d < 4:
            sent["t", "d", d - 1].wait_recv()
            k = PLACE[8 - d]
            if d < 3:
                send(("t", "d", d), tab.at[k, 0], tab.at[PLACE[7 - d], 0], z_down)
            send(("t", "c", 8 - d), tab.at[k, 0], tab.at[k, 1], mate)

    def places(t):
        masks = []
        for k in range(RING):
            named = jnp.concatenate([tab[k, 0, t, 0:8], tab[k, 1, t, 0:8]], axis=1)
            for j in range(2):
                hit = named == (2 * home + j).astype(F32)
                masks.append(jnp.sum(jnp.where(hit, 1.0, 0.0), axis=0, keepdims=True))
        mask = jnp.concatenate(masks, axis=0)
        before = lax.broadcasted_iota(jnp.int32, (256, 256), 0) < lax.broadcasted_iota(
            jnp.int32, (256, 256), 1
        )
        earlier = nn(mask.astype(BF), jnp.where(before, 1.0, 0.0).astype(BF))
        where = jnp.where(mask > 0.5, earlier, -1000.0)
        pos[t] = where
        turned = jnp.transpose(jnp.concatenate([where, jnp.zeros((112, 256), F32)], axis=0))
        for k in range(RING):
            post[t, k] = turned[:, 2 * k : 2 * k + 2]

    def chosen(t, k):
        slot = lax.broadcasted_iota(jnp.int32, (CAP, 256), 0).astype(F32)
        return [slot == pos[t, pl.ds(2 * k + j, 1)] for j in range(2)]

    def pick(t, src, dst, k):
        hot = jnp.concatenate([jnp.where(h, 1.0, 0.0) for h in chosen(t, k)], axis=0).astype(BF)
        got = nn(hot, src[k].reshape(256, D)).astype(BF)
        at = pl.ds(pl.multiple_of(k * CAP, 16), CAP)
        dst[0, at] = got[:CAP]
        dst[1, at] = got[CAP:]

    def pick_scales(t, k):
        named = jnp.concatenate([tab[k, 0, t, 0:8], tab[k, 1, t, 0:8]], axis=1)
        weight = jnp.concatenate([tab[k, 0, t, 8:16], tab[k, 1, t, 8:16]], axis=1)
        at = pl.ds(pl.multiple_of(k * CAP, 16), CAP)
        for j, h in enumerate(chosen(t, k)):
            mine = jnp.sum(
                jnp.where(named == (2 * home + j).astype(F32), weight, 0.0), axis=0, keepdims=True
            )
            ws[j, at] = jnp.sum(jnp.where(h, mine, 0.0), axis=1, keepdims=True)

    def pre(j, k0, n):
        at = pl.ds(k0 * CAP, n * CAP)
        x = xg[j, at]
        gp[j, at] = nn(x, wg[j])
        up[j, at] = nn(x, wu[j])

    def post_rows(j, k0, n):
        at = pl.ds(k0 * CAP, n * CAP)
        hidden = nt(gg[j, at], wd[j])
        gate = gp[j, at]
        sig = 1.0 / (1.0 + jnp.exp(-gate))
        hs = hidden * sig
        gate_grad = (hs * up[j, at] * (1.0 + gate * (1.0 - sig))).astype(BF)
        up_grad = (hs * gate).astype(BF)
        grown = nt(gate_grad, wg[j]) + nt(up_grad, wu[j])
        grown = (grown * ws[j, at]).astype(BF)
        for i in range(n):
            rw[k0 + i, j * CAP : (j + 1) * CAP] = grown[i * CAP : (i + 1) * CAP]

    def put(t, k):
        lane = lax.broadcasted_iota(jnp.int32, (256, 2 * CAP), 1).astype(F32)
        col = post[t, k]
        hot = jnp.logical_or(lane == col[:, 0:1], lane == col[:, 1:2] + float(CAP))
        summed = nn(jnp.where(hot, 1.0, 0.0).astype(BF), rw[k])
        part[t, k] = summed.astype(BF).reshape(2, TOK, D)

    def give_mate(t, d):
        k = PLACE[d]
        send((t, "rc", d), part.at[t, k, 1], l_core.at[t, k], mate)

    def give(t, way, d, ch):
        src = PLACE[d]
        if way == "d":
            send((t, "rd", d, ch), part.at[t, src, 0, rows(ch)], l_down.at[t, d - 1, rows(ch)], z_down)
        else:
            i = 7 - d
            send((t, "ru", d, ch), part.at[t, src, 0, rows(ch)], l_up.at[t, i, rows(ch)], z_up)

    def add_up(t, way, d, ch, arrived):
        k = PLACE[d]
        value = part[t, k, 0, rows(ch)].astype(F32) + l_core[t, k, rows(ch)].astype(F32)
        if arrived:
            landed = l_down[t, d, rows(ch)] if way == "d" else l_up[t, 8 - d, rows(ch)]
            value = value + landed.astype(F32)
        part[t, k, 0, rows(ch)] = value.astype(BF)

    def scatter_far(t):
        sent[t, "rc", 4].wait_recv()
        for way, ch in (("d", 0), ("u", 1)):
            add_up(t, way, 4, ch, False)
            give(t, way, 4, ch)

    def scatter_open(t):
        for way, d, ch in (("d", 3, 1), ("u", 5, 0)):
            sent[t, "rc", d].wait_recv()
            add_up(t, way, d, ch, False)
            give(t, way, d, ch)

    def scatter_step(t, n):
        turns = ((0, 1),) if n == 3 else ((1, 0), (0, 1))
        if n != 3:
            sent[t, "rc", n].wait_recv()
            sent[t, "rc", 8 - n].wait_recv()
        for ch_d, ch_u in turns:
            for way, d, ch in (("d", n, ch_d), ("u", 8 - n, ch_u)):
                back = d + 1 if way == "d" else d - 1
                sent[t, "r" + way, back, ch].wait_recv()
                add_up(t, way, d, ch, True)
                give(t, way, d, ch)

    def scatter_last(t, ch, own):
        sent[t, "rd", 1, ch].wait_recv()
        sent[t, "ru", 7, ch].wait_recv()
        at = rows(ch)
        return (
            own[0, 0, at].astype(F32)
            + (part[t, 0, 0, at].astype(F32) + l_core[t, 0, at].astype(F32))
            + (l_down[t, 0, at].astype(F32) + l_up[t, 0, at].astype(F32))
        ).astype(BF)

    def each(body):
        def step(k, carry):
            body(k)
            return carry

        lax.fori_loop(0, RING, step, 0)

    entered("t")
    table_step(0)
    entered("x0")
    for ch in range(2):
        gather_first("x0", x0, ch)
    entered("g0")
    for ch in range(2):
        gather_first("g0", g0, ch)
    first = (("x0", x0), ("g0", g0))
    for d in (1, 2, 3, 4):
        table_step(d)
        gather_step(first, d)
        if d == 3:
            entered("x1")
            for ch in range(2):
                gather_first("x1", x1, ch)
    for d in range(RING):
        sent["t", "c", d].wait_recv()
        gathered("x0", d)
        gathered("g0", d)
    second = (("x1", x1),)
    gather_step(second, 1)
    places(0)
    places(1)

    def pick0(k):
        pick(0, x0, xg, k)
        pick(0, g0, gg, k)
        pick_scales(0, k)

    each(pick0)
    gather_step(second, 2)
    for w in ("wg", "wu", "wd"):
        entered((w, 0))
    pre(0, 0, 8)
    gather_step(second, 3)
    for k0, n in ((0, 4), (4, 4)):
        post_rows(0, k0, n)
    gather_step(second, 4)
    entered(("wg", 1))
    entered(("wu", 1))
    pre(1, 0, 8)
    entered(("wd", 1))
    batches = ((7, 1, (4,)), (5, 2, (3, 5)), (3, 2, (2, 6)), (0, 3, (0, 1, 7)))
    for k0, n, ds in batches:
        post_rows(1, k0, n)
        for d in ds:
            put(0, PLACE[d])
            give_mate(0, d)
        if k0 == 5:
            scatter_far(0)
    scatter_open(0)
    for d in range(RING):
        gathered("x1", d)
    each(lambda k: pick(1, x1, xg, k))
    each(lambda k: pick_scales(1, k))
    scatter_step(0, 3)
    pre(0, 0, 8)
    scatter_step(0, 2)
    pre(1, 0, 8)
    scatter_step(0, 1)
    sent[0, "rc", 0].wait_recv()
    for ch in range(2):
        tot[0, rows(ch)] = scatter_last(0, ch, g0)
        send(("pass", ch), tot.at[0, rows(ch)], g1.at[0, 0, rows(ch)], pass_to)

    for ch in range(2):
        sent["pass", ch].wait_recv()
        gather_first("g1", g1, ch)
    third = (("g1", g1),)
    for d in (1, 2, 3, 4):
        gather_step(third, d)
        if d == 1:
            ds = (0,)
        elif d == 2:
            ds = (1, 7)
        elif d == 3:
            ds = (2, 6)
        else:
            ds = (3, 5)
        for q in ds:
            gathered("g1", q)
            pick(1, g1, gg, PLACE[q])
        if d > 1:
            k0, n = {2: (0, 3), 3: (3, 2), 4: (5, 2)}[d]
            for j in range(2):
                post_rows(j, k0, n)
            for q in (0, 1, 7) if d == 2 else ds:
                put(1, PLACE[q])
                give_mate(1, q)
    gathered("g1", 4)
    pick(1, g1, gg, 7)
    for j in range(2):
        post_rows(j, 7, 1)
    put(1, 7)
    give_mate(1, 4)
    scatter_open(1)
    scatter_far(1)
    scatter_step(1, 3)
    scatter_step(1, 2)
    scatter_step(1, 1)
    sent[1, "rc", 0].wait_recv()
    finals = []
    for ch in range(2):
        tot[1, rows(ch)] = scatter_last(1, ch, g1)
        enter(("fin", ch), tot.at[1, rows(ch)], fin.at[rows(ch)])
    for ch in range(2):
        entered(("fin", ch))
    out_ref[...] = fin[...]

    for copy in sent.values():
        copy.wait_send()

    @pl.when(mixed)
    def _():
        for _, copy in moves.values():
            copy.wait_send()


def shards(grad_out, saved_inputs, routes, gate_weights, w_gate, w_up, w_down):
    table = jnp.concatenate(
        [
            jnp.swapaxes(routes[0], 1, 2).astype(F32),
            jnp.swapaxes(gate_weights[0], 1, 2),
        ],
        axis=1,
    )
    block = pltpu.VMEM((RING, 2, TOK, D), BF)
    return pl.pallas_call(
        kernel,
        out_shape=jax.ShapeDtypeStruct((TOK, D), BF),
        in_specs=[pl.BlockSpec(memory_space=pl.ANY)] * 6,
        out_specs=pl.BlockSpec(memory_space=pltpu.VMEM),
        scratch_shapes=[
            block, block, block, block,
            pltpu.VMEM((RING, 2, 2, 16, TOK), F32),
            pltpu.VMEM((2, D, H), BF),
            pltpu.VMEM((2, D, H), BF),
            pltpu.VMEM((2, H, D), BF),
            pltpu.VMEM((2, RING, 2, TOK, D), BF),
            pltpu.VMEM((2, RING, TOK, D), BF),
            pltpu.VMEM((2, 4, TOK, D), BF),
            pltpu.VMEM((2, 4, TOK, D), BF),
            pltpu.VMEM((2, TOK, D), BF),
            pltpu.VMEM((TOK, D), BF),
            pltpu.VMEM((2, RING * CAP, D), BF),
            pltpu.VMEM((2, RING * CAP, D), BF),
            pltpu.VMEM((2, RING * CAP, H), F32),
            pltpu.VMEM((2, RING * CAP, H), F32),
            pltpu.VMEM((RING, 2 * CAP, D), BF),
            pltpu.VMEM((2, RING * CAP, 1), F32),
            pltpu.VMEM((2, 16, 256), F32),
            pltpu.VMEM((2, RING, 256, 2), F32),
            pltpu.SemaphoreType.DMA((SEMS,)),
            pltpu.SemaphoreType.DMA((SEMS,)),
            pltpu.SemaphoreType.DMA((16,)),
        ],
        compiler_params=pltpu.CompilerParams(
            collective_id=0, has_side_effects=True, vmem_limit_bytes=63 << 20
        ),
        name="moe_back",
    )(grad_out[0], saved_inputs[0], table, w_gate[0], w_up[0], w_down[0])[None]


def solution(mesh):
    placed = (
        P("section", "expert", None),
        P("section", None, "expert", None),
        P("section", None, "expert", None),
        P("section", None, "expert", None),
        P("section", "expert", None, None),
        P("section", "expert", None, None),
        P("section", "expert", None, None),
    )
    return jax.shard_map(
        shards, mesh=mesh, in_specs=placed, out_specs=P("section", "expert", None), check_vma=False
    )
```

time: 521 us -> 184 us (0.35); the launches traced: 513 us -> 184 us
  waiting for transfers between devices: 209 us -> 0 us
  Pallas kernels: 0 us -> 181 us
  blocking collectives: 132 us -> 0 us
  local copies, waits for them, and re-layouts: 60.9 us -> 1.67 us
  matrix products: 52.5 us -> 0 us
  other arithmetic: 33.7 us -> 2 us
  starting transfers between devices: 24.1 us -> 0 us
    all_to_all x4 -> x0, waiting for transfers between devices: 208 us -> none  [the longest x2 100 us: shards(): lax.all_to_all(row_grad, 'expert', split_axis=0, concat_axis=0, tiled=True)]
    pallas_call x0 -> x1, Pallas kernels: none -> 181 us  [shards(): pl.pallas_call(kernel, out_shape=jax.ShapeDtypeStruct((TOK, D), BF), in_s...]
    all_to_all x2 -> x0, blocking collectives: 132 us -> none  [the longest x1 70.5 us: shards(): lax.all_to_all(input_rows, 'expert', split_axis=0, concat_axis=0, tiled=T...]
    dot_general x8 -> x0, matrix products: 52.5 us -> none  [the longest x2 19.3 us: shards(): jnp.einsum('sjmh,jdh->sjmd', gate_grad, gate_local, preferred_element_typ...]
    gather x6 -> x0, local copies, waits for them, and re-layouts: 36.6 us -> none  [the longest x4 20.4 us: pack(): source[slot_token]]
    all_to_all x4 -> x0, starting transfers between devices: 21.6 us -> none  [the longest x2 12.2 us: shards(): lax.all_to_all(row_grad, 'expert', split_axis=0, concat_axis=0, tiled=True)]
    another operation x6 -> x0, other arithmetic: 18.3 us -> none
    scatter x4 -> x0, local copies, waits for them, and re-layouts: 17.5 us -> none  [the longest x2 8.85 us: layout(): jnp.zeros((expert_total * MOST,), jnp.int32).at[slot_index].set(1)]
  transfers between devices with their start and end apart: 5 -> 0, of which waited for: 5 -> 0; matrix products, arithmetic and copies ran while one was open for 7% -> 0% of each run, Pallas kernels for 0% -> 0%
where the time goes in v1:
time: 184 us
  Pallas kernels  181 us (98%)
  other arithmetic  2 us (1%)
    pallas_call x1, Pallas kernels, shards(): pl.pallas_call(kernel, out_shape=jax.ShapeDtypeStruct((TOK, D), BF), in_s...  181 us

profile of v1, /device:TPU:1, one launch (start us, length us, event | category | flops | bytes accessed | tf_op | source)
XLA Modules:
  0.0 184.2 jit_solution(8771364625923978387)
XLA Ops:
  0.0 0.7 convert_bitcast_fusion
  0.7 1.3 pad_maximum_fusion.table_in
  2.0 180.5 %moe_back.1 = bf16[128,1024]{1,0:T(8,128)(2,1)} custom-call(bf16[128,1024]{1,0:T(8,128)(2,1)} %bitcast.18, bf16[2,128,1024]{2,1,0:T(8,128)(2,1)} %bitcast.17, f32[2,16,128]{2,1,0:T(8,128)} %pad_maximum_fusion.table_in, bf16[2,1024,512]{2,1,0:T(8,128)(2,1)} %bitcast.13, bf16[2,1024,512]{2,1,0:T(8,128)(2,1)} %bitcast.14, bf16[2,512,1024]{2,1,0:T(8,128)(2,1)} %bitcast.15), custom_call_target="tpu_custom_call" | custom-call | tf_op jit(solution)/shard_map/moe_back/pallas_call | solution.py:407
  182.5 1.7 copy.9

commit v2 on v1

v2 whole, which is shorter than its diff:
```python
import jax
import jax.numpy as jnp
from jax import lax
from jax.experimental import pallas as pl
from jax.experimental.pallas import tpu as pltpu
from jax.sharding import PartitionSpec as P

BF = jnp.bfloat16
F32 = jnp.float32
TOK = 128
D = 1024
H = 512
CAP = 80
RING = 8
PLACE = {0: 0, 1: 1, 7: 2, 2: 3, 6: 4, 3: 5, 5: 6, 4: 7}
SENDERS = 40
TAKERS = 190


def nt(a, b):
    return lax.dot_general(a, b, (((1,), (1,)), ((), ())), preferred_element_type=F32)


def nn(a, b):
    return lax.dot_general(a, b, (((1,), (0,)), ((), ())), preferred_element_type=F32)


def kernel(
    grad_in, saved_in, routes_in, weights_in, wg_in, wu_in, wd_in, out_ref,
    xg0, x1, g1, tab, wg, wu, wd, part, l_core, l_down, l_up, tot, fin,
    xg, gg, gp, up, rw, ws, pos, post, own_routes, own_table, ssem, rsem, lsem,
):
    s = lax.axis_index("section")
    e = lax.axis_index("expert")
    core = lax.rem(s, 2)
    x_lo = lax.rem(e, 2)
    mixed = core != x_lo
    other_core = s + 1 - 2 * core
    other_x = e + 1 - 2 * x_lo
    z_up = (s, lax.rem(e + 2, 16))
    z_down = (s, lax.rem(e + 14, 16))
    mate = (other_core, e)
    swap = (other_core, other_x)
    pass_to = (lax.rem(s + 16 - 2 * (1 - x_lo), 16), other_x)
    pass_from = (lax.rem(s + 2 * x_lo, 16), other_x)
    home = lax.select(mixed, other_x, e)

    barrier = pltpu.get_barrier_semaphore()
    for peer in (z_up, z_down, mate, swap, pass_to, pass_from):
        pl.semaphore_signal(barrier, inc=1, device_id=peer, device_id_type=pl.DeviceIdType.MESH)

    senders, takers, sent, ends = {}, {}, {}, []

    def number(table, key):
        return table.setdefault(key, len(table))

    def make(batch, group, src, dst, peer):
        return pltpu.make_async_remote_copy(
            src_ref=src, dst_ref=dst,
            send_sem=ssem.at[number(senders, batch)], recv_sem=rsem.at[number(takers, group)],
            device_id=peer, device_id_type=pl.DeviceIdType.MESH,
        )

    def send(key, src, dst, peer, batch):
        sent[key] = make(batch, key, src, dst, peer)
        sent[key].start()

    moves = {}

    def enter(key, pairs, whole):
        i = number(moves, key)

        @pl.when(jnp.logical_not(mixed))
        def _():
            for src, dst in pairs:
                pltpu.make_async_copy(src, dst, lsem.at[i]).start()

        @pl.when(mixed)
        def _():
            for src, dst in pairs:
                make(key, key, src, dst, swap).start()

        ends.append((key, whole))

    def entered(key):
        whole = dict(ends)[key]

        @pl.when(jnp.logical_not(mixed))
        def _():
            pltpu.make_async_copy(whole, whole, lsem.at[moves[key]]).wait()

        @pl.when(mixed)
        def _():
            make(key, key, whole, whole, swap).wait_recv()

    loads = [
        pltpu.make_async_copy(routes_in, own_routes, lsem.at[18]),
        pltpu.make_async_copy(weights_in, own_table.at[:, 8:16], lsem.at[19]),
    ]
    for load in loads:
        load.start()
    pl.semaphore_wait(barrier, 6)
    for ch in range(2):
        at = pl.ds(64 * ch, 64)
        enter(
            ("a", ch),
            [
                (saved_in.at[0, at], xg0.at[0, 0, 0, at]),
                (grad_in.at[at], xg0.at[0, 0, 1, at]),
            ],
            xg0.at[0, 0, :, at],
        )
    for load in loads:
        load.wait()
    own_table[:, 0:8] = own_routes[...].astype(F32)
    enter("t", [(own_table, tab.at[0, 0])], tab.at[0, 0])
    for j in range(2):
        for name, src, dst in (("wg", wg_in, wg), ("wu", wu_in, wu), ("wd", wd_in, wd)):
            enter((name, j), [(src.at[j], dst.at[j])], dst.at[j])
        if j == 0:
            enter("x1", [(saved_in.at[1], x1.at[0, 0])], x1.at[0, 0])

    def rows(ch, n):
        return pl.ds(TOK // n * ch, TOK // n)

    def upper(ch, n):
        return ch < n // 2

    def piece(buf, k, c, at):
        return buf.at[k, c, :, at] if len(buf.shape) == 5 else buf.at[k, c, at]

    def to_mate(name, buf, d, ch, n):
        k = PLACE[d]
        at = rows(ch, n)
        make((name, "c"), (name, "c", d), piece(buf, k, 0, at), piece(buf, k, 1, at), mate).start()

    def gathered(name, buf, d):
        k = PLACE[d]
        make((name, "c"), (name, "c", d), buf.at[k, 0], buf.at[k, 1], mate).wait_recv()

    def hop(name, buf, way, d, ch, n):
        src, dst = (d, d + 1) if way == "u" else ((8 - d) % 8, 7 - d)
        at = rows(ch, n)
        send(
            (name, way, d, ch),
            piece(buf, PLACE[src], 0, at),
            piece(buf, PLACE[dst], 0, at),
            z_up if way == "u" else z_down,
            (name, "z"),
        )

    def gather_first(name, buf, ch, n):
        hop(name, buf, "u", 0, ch, n)
        hop(name, buf, "d", 0, ch, n)
        to_mate(name, buf, 0, ch, n)

    def gather_step(name, buf, d, chs, n):
        for ch in chs:
            for way in "ud":
                here = d if way == "u" else 8 - d
                half = (way == "u") == upper(ch, n)
                if d < 4 or half:
                    sent[name, way, d - 1, ch].wait_recv()
                    if d < 3 or (d == 3 and half):
                        hop(name, buf, way, d, ch, n)
                    to_mate(name, buf, here, ch, n)

    def table_step(d):
        def on(way, d, k, to, peer):
            send(("t", way, d), tab.at[k, 0], tab.at[to, 0], peer, ("t", "z"))

        def across(d, k):
            make(("t", "c"), ("t", "c"), tab.at[k, 0], tab.at[k, 1], mate).start()

        if d == 0:
            on("u", 0, 0, PLACE[1], z_up)
            on("d", 0, 0, PLACE[7], z_down)
            across(0, 0)
            return
        sent["t", "u", d - 1].wait_recv()
        k = PLACE[d]
        if d < 4:
            on("u", d, k, PLACE[d + 1], z_up)
        across(d, k)
        if d < 4:
            sent["t", "d", d - 1].wait_recv()
            k = PLACE[8 - d]
            if d < 3:
                on("d", d, k, PLACE[7 - d], z_down)
            across(8 - d, k)

    def tables_there():
        make(("t", "c"), ("t", "c"), tab.at[:, 0], tab.at[:, 1], mate).wait_recv()

    def places(t):
        masks = []
        for k in range(RING):
            named = jnp.concatenate([tab[k, 0, t, 0:8], tab[k, 1, t, 0:8]], axis=1)
            for j in range(2):
                hit = named == (2 * home + j).astype(F32)
                masks.append(jnp.sum(jnp.where(hit, 1.0, 0.0), axis=0, keepdims=True))
        mask = jnp.concatenate(masks, axis=0)
        before = lax.broadcasted_iota(jnp.int32, (256, 256), 0) < lax.broadcasted_iota(
            jnp.int32, (256, 256), 1
        )
        earlier = nn(mask.astype(BF), jnp.where(before, 1.0, 0.0).astype(BF))
        where = jnp.where(mask > 0.5, earlier, -1000.0)
        pos[t] = where
        turned = jnp.transpose(jnp.concatenate([where, jnp.zeros((112, 256), F32)], axis=0))
        for k in range(RING):
            post[t, k] = turned[:, 2 * k : 2 * k + 2]

    def chosen(t, k):
        slot = lax.broadcasted_iota(jnp.int32, (CAP, 256), 0).astype(F32)
        return [slot == pos[t, pl.ds(2 * k + j, 1)] for j in range(2)]

    def pick(t, src, dst, k):
        hot = jnp.concatenate([jnp.where(h, 1.0, 0.0) for h in chosen(t, k)], axis=0).astype(BF)
        got = nn(hot, src.reshape(256, D)).astype(BF)
        at = pl.ds(pl.multiple_of(k * CAP, 16), CAP)
        dst[0, at] = got[:CAP]
        dst[1, at] = got[CAP:]

    def pick_scales(t, k):
        named = jnp.concatenate([tab[k, 0, t, 0:8], tab[k, 1, t, 0:8]], axis=1)
        weight = jnp.concatenate([tab[k, 0, t, 8:16], tab[k, 1, t, 8:16]], axis=1)
        at = pl.ds(pl.multiple_of(k * CAP, 16), CAP)
        for j, h in enumerate(chosen(t, k)):
            mine = jnp.sum(
                jnp.where(named == (2 * home + j).astype(F32), weight, 0.0), axis=0, keepdims=True
            )
            ws[j, at] = jnp.sum(jnp.where(h, mine, 0.0), axis=1, keepdims=True)

    def pre(j, k0, n):
        at = pl.ds(k0 * CAP, n * CAP)
        x = xg[j, at]
        gp[j, at] = nn(x, wg[j])
        up[j, at] = nn(x, wu[j])

    def post_rows(j, k0, n):
        at = pl.ds(k0 * CAP, n * CAP)
        hidden = nt(gg[j, at], wd[j])
        gate = gp[j, at]
        sig = 1.0 / (1.0 + jnp.exp(-gate))
        hs = hidden * sig
        gate_grad = (hs * up[j, at] * (1.0 + gate * (1.0 - sig))).astype(BF)
        up_grad = (hs * gate).astype(BF)
        grown = nt(gate_grad, wg[j]) + nt(up_grad, wu[j])
        grown = (grown * ws[j, at]).astype(BF)
        for i in range(n):
            rw[k0 + i, j * CAP : (j + 1) * CAP] = grown[i * CAP : (i + 1) * CAP]

    def put(t, k):
        lane = lax.broadcasted_iota(jnp.int32, (256, 2 * CAP), 1).astype(F32)
        col = post[t, k]
        hot = jnp.logical_or(lane == col[:, 0:1], lane == col[:, 1:2] + float(CAP))
        summed = nn(jnp.where(hot, 1.0, 0.0).astype(BF), rw[k])
        part[t, k] = summed.astype(BF).reshape(2, TOK, D)

    def give_mate(t, d):
        k = PLACE[d]
        send((t, "rc", d), part.at[t, k, 1], l_core.at[t, k], mate, (t, "rc"))

    def give(t, way, d, ch):
        src = part.at[t, PLACE[d], 0, rows(ch, 4)]
        if way == "d":
            send((t, "rd", d, ch), src, l_down.at[t, d - 1, rows(ch, 4)], z_down, (t, "rz"))
        else:
            send((t, "ru", d, ch), src, l_up.at[t, 7 - d, rows(ch, 4)], z_up, (t, "rz"))

    def add_up(t, way, d, ch, arrived):
        k = PLACE[d]
        at = rows(ch, 4)
        value = part[t, k, 0, at].astype(F32) + l_core[t, k, at].astype(F32)
        if arrived:
            landed = l_down[t, d, at] if way == "d" else l_up[t, 8 - d, at]
            value = value + landed.astype(F32)
        part[t, k, 0, at] = value.astype(BF)

    def scatter_open(t):
        sent[t, "rc", 3].wait_recv()
        sent[t, "rc", 5].wait_recv()
        for i in range(2):
            for way, d, ch in (("d", 3, 2 + i), ("u", 5, i)):
                add_up(t, way, d, ch, False)
                give(t, way, d, ch)

    def scatter_far(t):
        sent[t, "rc", 4].wait_recv()
        for i in range(2):
            for way, ch in (("d", i), ("u", 2 + i)):
                add_up(t, way, 4, ch, False)
                give(t, way, 4, ch)

    def scatter_step(t, n):
        turns = {3: ((0, 2), (1, 3)), 2: ((2, 0), (0, 2), (3, 1), (1, 3)), 1: ((0, 0), (2, 2), (1, 1), (3, 3))}[n]
        if n != 3:
            sent[t, "rc", n].wait_recv()
            sent[t, "rc", 8 - n].wait_recv()
        for ch_d, ch_u in turns:
            for way, d, ch in (("d", n, ch_d), ("u", 8 - n, ch_u)):
                back = d + 1 if way == "d" else d - 1
                sent[t, "r" + way, back, ch].wait_recv()
                add_up(t, way, d, ch, True)
                give(t, way, d, ch)

    def scatter_last(t, ch, own):
        sent[t, "rd", 1, ch].wait_recv()
        sent[t, "ru", 7, ch].wait_recv()
        at = rows(ch, 4)
        tot[t, at] = (
            own[at].astype(F32)
            + (part[t, 0, 0, at].astype(F32) + l_core[t, 0, at].astype(F32))
            + (l_down[t, 0, at].astype(F32) + l_up[t, 0, at].astype(F32))
        ).astype(BF)

    def each(body):
        def step(k, carry):
            body(k)
            return carry

        lax.fori_loop(0, RING, step, 0)

    for ch in range(2):
        entered(("a", ch))
        gather_first("a", xg0, ch, 2)
    entered("t")
    table_step(0)
    for d in (1, 2, 3, 4):
        gather_step("a", xg0, d, (0, 1), 2)
        table_step(d)
        if d == 3:
            entered("x1")
            for ch in range(2):
                gather_first("x1", x1, ch, 2)
    tables_there()
    places(0)
    places(1)
    for d in range(RING):
        gathered("a", xg0, d)
    gather_step("x1", x1, 1, (0, 1), 2)

    def pick0(k):
        pick(0, xg0[k, :, 0], xg, k)
        pick(0, xg0[k, :, 1], gg, k)
        pick_scales(0, k)

    each(pick0)
    gather_step("x1", x1, 2, (0, 1), 2)
    for w in ("wg", "wu", "wd"):
        entered((w, 0))
    pre(0, 0, 8)
    gather_step("x1", x1, 3, (0, 1), 2)
    for k0, n in ((0, 4), (4, 4)):
        post_rows(0, k0, n)
    gather_step("x1", x1, 4, (0, 1), 2)
    for d in range(RING):
        gathered("x1", x1, d)
    entered(("wg", 1))
    entered(("wu", 1))
    pre(1, 0, 8)
    each(lambda k: pick(1, x1[k], xg, k))
    entered(("wd", 1))

    def finish(t, ds):
        for d in ds:
            put(t, PLACE[d])
            give_mate(t, d)

    post_rows(1, 5, 3)
    finish(0, (3, 5, 4))
    post_rows(1, 3, 2)
    scatter_open(0)
    scatter_far(0)
    finish(0, (2, 6))
    post_rows(1, 0, 3)
    finish(0, (1, 7, 0))
    scatter_step(0, 3)
    pre(0, 0, 8)
    scatter_step(0, 2)
    pre(1, 0, 8)
    each(lambda k: pick_scales(1, k))
    scatter_step(0, 1)
    sent[0, "rc", 0].wait_recv()
    order = (0, 2, 1, 3)

    def passing(ch):
        scatter_last(0, ch, xg0.at[0, 0, 1])
        at = rows(ch, 4)
        send(("pass", ch), tot.at[0, at], g1.at[0, 0, at], pass_to, "pass")

    def passed(ch):
        sent["pass", ch].wait_recv()
        gather_first("g1", g1, ch, 4)

    passing(0)
    passing(2)
    passed(0)
    passing(1)
    passed(2)
    passing(3)
    passed(1)
    passed(3)

    def level(d, ch):
        gather_step("g1", g1, d, (ch,), 4)

    def take(ds):
        for d in ds:
            gathered("g1", g1, d)
            pick(1, g1[PLACE[d]], gg, PLACE[d])

    for ch in order:
        level(1, ch)
    take((0,))
    level(2, 0)
    level(2, 2)
    take((1, 7))
    level(2, 1)
    post_rows(0, 0, 3)
    level(2, 3)
    post_rows(1, 0, 3)
    level(3, 0)
    finish(1, (1, 7, 0))
    level(3, 2)
    take((2, 6))
    post_rows(0, 3, 2)
    level(3, 1)
    post_rows(1, 3, 2)
    level(3, 3)
    finish(1, (2, 6))
    level(4, 0)
    level(4, 2)
    take((3, 5))
    post_rows(0, 5, 2)
    level(4, 1)
    level(4, 3)
    post_rows(1, 5, 2)
    finish(1, (3, 5))
    take((4,))
    post_rows(0, 7, 1)
    scatter_open(1)
    post_rows(1, 7, 1)
    finish(1, (4,))
    scatter_far(1)
    scatter_step(1, 3)
    scatter_step(1, 2)
    scatter_step(1, 1)
    sent[1, "rc", 0].wait_recv()
    for ch in order:
        scatter_last(1, ch, g1.at[0, 0])
        enter(("fin", ch), [(tot.at[1, rows(ch, 4)], fin.at[rows(ch, 4)])], fin.at[rows(ch, 4)])
    for ch in order:
        entered(("fin", ch))
        out_ref[rows(ch, 4)] = fin[rows(ch, 4)]

    for name, buf in (("a", xg0), ("x1", x1), ("g1", g1), ("t", tab)):
        group = ("t", "c") if name == "t" else (name, "c", 0)
        make((name, "z"), group, buf.at[0:7, 0], buf.at[0:7, 1], z_up).wait_send()
        make((name, "c"), group, buf.at[:, 0], buf.at[:, 1], mate).wait_send()
    for t in range(2):
        make((t, "rz"), (t, "rc", 0), part.at[t, 0:7, 0], part.at[t, 0:7, 0], z_up).wait_send()
        make((t, "rc"), (t, "rc", 0), part.at[t, :, 1], part.at[t, :, 1], mate).wait_send()
    make("pass", ("pass", 0), tot.at[0], tot.at[0], pass_to).wait_send()

    @pl.when(mixed)
    def _():
        for key, whole in ends:
            make(key, key, whole, whole, swap).wait_send()

    assert len(senders) <= SENDERS and len(takers) <= TAKERS, (len(senders), len(takers))

def shards(grad_out, saved_inputs, routes, gate_weights, w_gate, w_up, w_down):
    block = pltpu.VMEM((RING, 2, TOK, D), BF)
    return pl.pallas_call(
        kernel,
        out_shape=jax.ShapeDtypeStruct((TOK, D), BF),
        in_specs=[pl.BlockSpec(memory_space=pl.ANY)] * 7,
        out_specs=pl.BlockSpec(memory_space=pltpu.VMEM),
        scratch_shapes=[
            pltpu.VMEM((RING, 2, 2, TOK, D), BF),
            block, block,
            pltpu.VMEM((RING, 2, 2, 16, TOK), F32),
            pltpu.VMEM((2, D, H), BF),
            pltpu.VMEM((2, D, H), BF),
            pltpu.VMEM((2, H, D), BF),
            pltpu.VMEM((2, RING, 2, TOK, D), BF),
            pltpu.VMEM((2, RING, TOK, D), BF),
            pltpu.VMEM((2, 4, TOK, D), BF),
            pltpu.VMEM((2, 4, TOK, D), BF),
            pltpu.VMEM((2, TOK, D), BF),
            pltpu.VMEM((TOK, D), BF),
            pltpu.VMEM((2, RING * CAP, D), BF),
            pltpu.VMEM((2, RING * CAP, D), BF),
            pltpu.VMEM((2, RING * CAP, H), F32),
            pltpu.VMEM((2, RING * CAP, H), F32),
            pltpu.VMEM((RING, 2 * CAP, D), BF),
            pltpu.VMEM((2, RING * CAP, 1), F32),
            pltpu.VMEM((2, 16, 256), F32),
            pltpu.VMEM((2, RING, 256, 2), F32),
            pltpu.VMEM((2, 8, TOK), jnp.int32),
            pltpu.VMEM((2, 16, TOK), F32),
            pltpu.SemaphoreType.DMA((SENDERS,)),
            pltpu.SemaphoreType.DMA((TAKERS,)),
            pltpu.SemaphoreType.DMA((20,)),
        ],
        compiler_params=pltpu.CompilerParams(
            collective_id=0, has_side_effects=True, vmem_limit_bytes=63 << 20
        ),
        name="moe_back",
    )(
        grad_out[0],
        saved_inputs[0],
        jnp.swapaxes(routes[0], 1, 2),
        jnp.swapaxes(gate_weights[0], 1, 2),
        w_gate[0],
        w_up[0],
        w_down[0],
    )[None]


def solution(mesh):
    placed = (
        P("section", "expert", None),
        P("section", None, "expert", None),
        P("section", None, "expert", None),
        P("section", None, "expert", None),
        P("section", "expert", None, None),
        P("section", "expert", None, None),
        P("section", "expert", None, None),
    )
    return jax.shard_map(
        shards, mesh=mesh, in_specs=placed, out_specs=P("section", "expert", None), check_vma=False
    )
```

time: 184 us -> 171 us (0.929)
  Pallas kernels: 181 us -> 170 us
  other arithmetic: 2 us -> 0 us
    pallas_call x1, Pallas kernels: 181 us -> 170 us  [shards(): pl.pallas_call(kernel, out_shape=jax.ShapeDtypeStruct((TOK, D), BF), in_s...]
where the time goes in v2:
time: 171 us
  Pallas kernels  170 us (99%)
    pallas_call x1, Pallas kernels, shards(): pl.pallas_call(kernel, out_shape=jax.ShapeDtypeStruct((TOK, D), BF), in_s...  170 us

profile of v2, /device:TPU:1, one launch (start us, length us, event | category | flops | bytes accessed | tf_op | source)
XLA Modules:
  0.0 171.2 jit_solution(15000772184260242294)
XLA Ops:
  0.0 169.5 %moe_back.1 = bf16[128,1024]{1,0:T(8,128)(2,1)} custom-call(bf16[128,1024]{1,0:T(8,128)(2,1)} %bitcast.17, bf16[2,128,1024]{2,1,0:T(8,128)(2,1)} %bitcast.16, s32[2,8,128]{2,1,0:T(8,128)} %bitcast.18, f32[2,8,128]{2,1,0:T(8,128)} %bitcast.19, bf16[2,1024,512]{2,1,0:T(8,128)(2,1)} %bitcast.12, bf16[2,1024,512]{2,1,0:T(8,128)(2,1)} %bitcast.13, ...), custom_call_target="tpu_custom_call" | custom-call | tf_op jit(solution)/shard_map/moe_back/pallas_call | solution.py:475
  169.5 1.7 copy.9

commit v3 on v2

v3 whole, which is shorter than its diff:
```python
import jax
import jax.numpy as jnp
from jax import lax
from jax.experimental import pallas as pl
from jax.experimental.pallas import tpu as pltpu
from jax.sharding import PartitionSpec as P

BF = jnp.bfloat16
F32 = jnp.float32
TOK = 128
D = 1024
H = 512
CAP = 80
RING = 8
PLACE = {0: 0, 1: 1, 7: 2, 2: 3, 6: 4, 3: 5, 5: 6, 4: 7}
SENDERS = 40
TAKERS = 162
FINE = 8


def nt(a, b):
    return lax.dot_general(a, b, (((1,), (1,)), ((), ())), preferred_element_type=F32)


def nn(a, b):
    return lax.dot_general(a, b, (((1,), (0,)), ((), ())), preferred_element_type=F32)


def kernel(
    grad_in, saved_in, routes_in, weights_in, wg_in, wu_in, wd_in, out_ref,
    xg0, x1, g1, tab, wg, wu, wd, part, l_core, l_down, l_up, tot,
    xg, gg, gp, up, rw, ws, pos_full, post_full, pos_half, post_half, own_routes, own_table, ssem, rsem, lsem,
):
    s = lax.axis_index("section")
    e = lax.axis_index("expert")
    core = lax.rem(s, 2)
    x_lo = lax.rem(e, 2)
    mixed = core != x_lo
    other_core = s + 1 - 2 * core
    other_x = e + 1 - 2 * x_lo
    z_up = (s, lax.rem(e + 2, 16))
    z_down = (s, lax.rem(e + 14, 16))
    mate = (other_core, e)
    swap = (other_core, other_x)
    pass_to = (lax.rem(s + 16 - 2 * (1 - x_lo), 16), other_x)
    pass_from = (lax.rem(s + 2 * x_lo, 16), other_x)
    home = lax.select(mixed, other_x, e)

    barrier = pltpu.get_barrier_semaphore()
    for peer in (z_up, z_down, mate, swap, pass_to, pass_from):
        pl.semaphore_signal(barrier, inc=1, device_id=peer, device_id_type=pl.DeviceIdType.MESH)

    senders, takers, sent, ends = {}, {}, {}, []

    def number(table, key):
        return table.setdefault(key, len(table))

    def make(batch, group, src, dst, peer):
        if group[0] == 1:
            group = (0,) + group[1:]
        elif group[0] == "g1" and group[1] == "c":
            group = ("a",) + group[1:]
        elif group[0] == "g1":
            place = 4 if group[2] == 3 else 3 - group[2]
            group = (0, "r" + group[1], place if group[1] == "d" else 8 - place, group[3])
        return pltpu.make_async_remote_copy(
            src_ref=src, dst_ref=dst,
            send_sem=ssem.at[number(senders, batch)], recv_sem=rsem.at[number(takers, group)],
            device_id=peer, device_id_type=pl.DeviceIdType.MESH,
        )

    def send(key, src, dst, peer, batch):
        sent[key] = make(batch, key, src, dst, peer)
        sent[key].start()

    moves = {}

    def enter(key, pairs, whole):
        i = number(moves, key)

        @pl.when(jnp.logical_not(mixed))
        def _():
            for src, dst in pairs:
                pltpu.make_async_copy(src, dst, lsem.at[i]).start()

        @pl.when(mixed)
        def _():
            for src, dst in pairs:
                make(key, key, src, dst, swap).start()

        ends.append((key, whole))

    def entered(key):
        whole = dict(ends)[key]

        @pl.when(jnp.logical_not(mixed))
        def _():
            pltpu.make_async_copy(whole, whole, lsem.at[moves[key]]).wait()

        @pl.when(mixed)
        def _():
            make(key, key, whole, whole, swap).wait_recv()

    loads = [
        pltpu.make_async_copy(routes_in, own_routes, lsem.at[18]),
        pltpu.make_async_copy(weights_in, own_table.at[:, 8:16], lsem.at[19]),
    ]
    for load in loads:
        load.start()
    pl.semaphore_wait(barrier, 6)
    for ch in range(2):
        at = pl.ds(64 * ch, 64)
        enter(
            ("a", ch),
            [
                (saved_in.at[0, at], xg0.at[0, 0, 0, at]),
                (grad_in.at[at], xg0.at[0, 0, 1, at]),
            ],
            xg0.at[0, 0, :, at],
        )
    for load in loads:
        load.wait()
    own_table[:, 0:8] = own_routes[...].astype(F32)
    enter("t", [(own_table, tab.at[0, 0])], tab.at[0, 0])
    for j in range(2):
        for name, src, dst in (("wg", wg_in, wg), ("wu", wu_in, wu), ("wd", wd_in, wd)):
            enter((name, j), [(src.at[j], dst.at[j])], dst.at[j])
        if j == 0:
            enter("x1", [(saved_in.at[1], x1.at[0, 0])], x1.at[0, 0])

    def rows(ch, n):
        return pl.ds(TOK // n * ch, TOK // n)

    def upper(ch, n):
        return ch % 2 == 0 if n == 2 else ch // 2 % 2 == 0

    def piece(buf, k, c, at):
        return buf.at[k, c, :, at] if len(buf.shape) == 5 else buf.at[k, c, at]

    def to_mate(name, buf, d, ch, n):
        k = PLACE[d]
        at = rows(ch, n)
        group = (name, "c", d, 2 * ch // n if n == FINE else 0)
        make((name, "c"), group, piece(buf, k, 0, at), piece(buf, k, 1, at), mate).start()

    def gathered(name, buf, d, h=0, at=pl.ds(0, TOK)):
        k = PLACE[d]
        group = (name, "c", d, h)
        make((name, "c"), group, piece(buf, k, 0, at), piece(buf, k, 1, at), mate).wait_recv()

    def hop(name, buf, way, d, ch, n):
        src, dst = (d, d + 1) if way == "u" else ((8 - d) % 8, 7 - d)
        at = rows(ch, n)
        send(
            (name, way, d, ch),
            piece(buf, PLACE[src], 0, at),
            piece(buf, PLACE[dst], 0, at),
            z_up if way == "u" else z_down,
            (name, "z"),
        )

    def gather_first(name, buf, ch, n):
        hop(name, buf, "u", 0, ch, n)
        hop(name, buf, "d", 0, ch, n)
        to_mate(name, buf, 0, ch, n)

    def gather_step(name, buf, d, chs, n):
        for pair in chs:
            for way, ch in zip("ud", pair):
                here = d if way == "u" else 8 - d
                half = (way == "u") == upper(ch, n)
                if d < 4 or half:
                    sent[name, way, d - 1, ch].wait_recv()
                    if d < 3 or (d == 3 and half):
                        hop(name, buf, way, d, ch, n)
                    to_mate(name, buf, here, ch, n)

    def table_step(d):
        def on(way, d, k, to, peer):
            send(("t", way, d), tab.at[k, 0], tab.at[to, 0], peer, ("t", "z"))

        def across(d, k):
            make(("t", "c"), ("t", "c"), tab.at[k, 0], tab.at[k, 1], mate).start()

        if d == 0:
            on("u", 0, 0, PLACE[1], z_up)
            on("d", 0, 0, PLACE[7], z_down)
            across(0, 0)
            return
        sent["t", "u", d - 1].wait_recv()
        k = PLACE[d]
        if d < 4:
            on("u", d, k, PLACE[d + 1], z_up)
        across(d, k)
        if d < 4:
            sent["t", "d", d - 1].wait_recv()
            k = PLACE[8 - d]
            if d < 3:
                on("d", d, k, PLACE[7 - d], z_down)
            across(8 - d, k)

    def tables_there():
        make(("t", "c"), ("t", "c"), tab.at[:, 0], tab.at[:, 1], mate).wait_recv()

    def half(h):
        return pl.ds(0, TOK) if h is None else pl.ds(64 * h, 64)

    def lanes(k, t, h, first):
        both = [tab[k, c, t, first : first + 8] for c in range(2)]
        if h is not None:
            both = [v[:, 64 * h : 64 * h + 64] for v in both]
        return jnp.concatenate(both, axis=1)

    def places(t, h, pos, post):
        masks = []
        for k in range(RING):
            named = lanes(k, t, h, 0)
            for j in range(2):
                hit = named == (2 * home + j).astype(F32)
                masks.append(jnp.sum(jnp.where(hit, 1.0, 0.0), axis=0, keepdims=True))
        mask = jnp.concatenate(masks, axis=0)
        n = mask.shape[1]
        before = lax.broadcasted_iota(jnp.int32, (n, n), 0) < lax.broadcasted_iota(
            jnp.int32, (n, n), 1
        )
        earlier = nn(mask.astype(BF), jnp.where(before, 1.0, 0.0).astype(BF))
        where = jnp.where(mask > 0.5, earlier, -1000.0)
        pos[...] = where
        turned = jnp.transpose(jnp.concatenate([where, jnp.zeros((112, n), F32)], axis=0))
        for k in range(RING):
            post[k] = turned[:, 2 * k : 2 * k + 2]

    def chosen(pos, k):
        slot = lax.broadcasted_iota(jnp.int32, (CAP, pos.shape[1]), 0).astype(F32)
        return [slot == pos[pl.ds(2 * k + j, 1)] for j in range(2)]

    def unit_rows(k):
        return pl.ds(pl.multiple_of(k * CAP, 16), CAP)

    def pos_of(h):
        return pos_full if h is None else pos_half.at[h]

    def pick(h, tokens, dst, k):
        pos = pos_of(h)
        hot = jnp.concatenate([jnp.where(c, 1.0, 0.0) for c in chosen(pos, k)], axis=0).astype(BF)
        got = nn(hot, tokens.reshape(pos.shape[1], D)).astype(BF)
        dst[0, unit_rows(k)] = got[:CAP]
        dst[1, unit_rows(k)] = got[CAP:]

    def pick_scales(t, h, k):
        named = lanes(k, t, h, 0)
        weight = lanes(k, t, h, 8)
        for j, hit in enumerate(chosen(pos_of(h), k)):
            mine = jnp.sum(
                jnp.where(named == (2 * home + j).astype(F32), weight, 0.0), axis=0, keepdims=True
            )
            ws[t + (h or 0), j, unit_rows(k)] = jnp.sum(jnp.where(hit, mine, 0.0), axis=1, keepdims=True)

    def pre(h, j):
        x = xg[j]
        gp[h, j] = nn(x, wg[j])
        up[h, j] = nn(x, wu[j])

    def post_rows(t, h, j, k0, n):
        at = pl.ds(k0 * CAP, n * CAP)
        hidden = nt(gg[j, at], wd[j])
        gate = gp[h, j, at]
        sig = 1.0 / (1.0 + jnp.exp(-gate))
        hs = hidden * sig
        gate_grad = (hs * up[h, j, at] * (1.0 + gate * (1.0 - sig))).astype(BF)
        up_grad = (hs * gate).astype(BF)
        grown = nt(gate_grad, wg[j]) + nt(up_grad, wu[j])
        grown = (grown * ws[t + h, j, at]).astype(BF)
        for i in range(n):
            rw[k0 + i, j * CAP : (j + 1) * CAP] = grown[i * CAP : (i + 1) * CAP]

    def put(t, h, k):
        col = post_full[k] if h is None else post_half[h, k]
        lane = lax.broadcasted_iota(jnp.int32, (col.shape[0], 2 * CAP), 1).astype(F32)
        hot = jnp.logical_or(lane == col[:, 0:1], lane == col[:, 1:2] + float(CAP))
        summed = nn(jnp.where(hot, 1.0, 0.0).astype(BF), rw[k]).astype(BF)
        part[t, k, :, half(h)] = summed.reshape(2, col.shape[0] // 2, D)

    def halved(t, h, d):
        return h if t == 1 else None

    def give_mate(t, h, d):
        k = PLACE[d]
        h = halved(t, h, d)
        at = half(h)
        send((t, "rc", d, h or 0), part.at[t, k, 1, at], l_core.at[t, k, at], mate, (t, "rc"))

    there = set()

    def mate_there(t, h, *ds):
        for d in ds:
            key = (t, "rc", d, halved(t, h, d) or 0)
            if key not in there:
                there.add(key)
                sent[key].wait_recv()

    def give(t, way, d, ch):
        src = part.at[t, PLACE[d], 0, rows(ch, FINE)]
        if way == "d":
            send((t, "rd", d, ch), src, l_down.at[t, d - 1, rows(ch, FINE)], z_down, (t, "rz"))
        else:
            send((t, "ru", d, ch), src, l_up.at[t, 7 - d, rows(ch, FINE)], z_up, (t, "rz"))

    def add_up(t, way, d, ch, arrived):
        k = PLACE[d]
        at = rows(ch, FINE)
        value = part[t, k, 0, at].astype(F32) + l_core[t, k, at].astype(F32)
        if arrived:
            landed = l_down[t, d, at] if way == "d" else l_up[t, 8 - d, at]
            value = value + landed.astype(F32)
        part[t, k, 0, at] = value.astype(BF)

    def far(t, h):
        mate_there(t, h, 4)
        for i in range(2):
            for way, ch in (("d", 4 * h + i), ("u", 4 * h + 2 + i)):
                add_up(t, way, 4, ch, False)
                give(t, way, 4, ch)

    def near(t, h):
        mate_there(t, h, 3, 5)
        for i in range(2):
            for way, d, ch in (("d", 3, 4 * h + 2 + i), ("u", 5, 4 * h + i)):
                add_up(t, way, d, ch, False)
                give(t, way, d, ch)

    def step(t, n, quarter_d, quarter_u):
        mate_there(t, quarter_d // 2, n, 8 - n)
        for i in range(2):
            for way, d, ch in (("d", n, 2 * quarter_d + i), ("u", 8 - n, 2 * quarter_u + i)):
                back = d + 1 if way == "d" else d - 1
                sent[t, "r" + way, back, ch].wait_recv()
                add_up(t, way, d, ch, True)
                give(t, way, d, ch)

    def scatter_last(t, ch, own):
        mate_there(t, ch // 4, 0)
        sent[t, "rd", 1, ch].wait_recv()
        sent[t, "ru", 7, ch].wait_recv()
        at = rows(ch, FINE)
        tot[t, at] = (
            own[at].astype(F32)
            + (part[t, 0, 0, at].astype(F32) + l_core[t, 0, at].astype(F32))
            + (l_down[t, 0, at].astype(F32) + l_up[t, 0, at].astype(F32))
        ).astype(BF)

    def each(body, first=0, last=RING):
        def turn(k, carry):
            body(k)
            return carry

        lax.fori_loop(first, last, turn, 0)

    both = ((0, 0), (1, 1))
    for ch in range(2):
        entered(("a", ch))
        gather_first("a", xg0, ch, 2)
    entered("t")
    table_step(0)
    for d in (1, 2, 3, 4):
        gather_step("a", xg0, d, both, 2)
        table_step(d)
        if d == 3:
            entered("x1")
            for ch in range(2):
                gather_first("x1", x1, ch, 2)
    tables_there()
    places(0, None, pos_full, post_full)
    for h in range(2):
        places(1, h, pos_half.at[h], post_half.at[h])
    for d in range(RING):
        gathered("a", xg0, d)
    gather_step("x1", x1, 1, both, 2)

    def pick0(k):
        pick(None, xg0[k, :, 0], xg, k)
        pick(None, xg0[k, :, 1], gg, k)
        pick_scales(0, None, k)

    each(pick0)
    gather_step("x1", x1, 2, both, 2)
    for w in ("wg", "wu", "wd"):
        entered((w, 0))
    pre(0, 0)
    gather_step("x1", x1, 3, both, 2)
    for u0 in (0, 4):
        post_rows(0, 0, 0, u0, 4)
    gather_step("x1", x1, 4, both, 2)
    for d in range(RING):
        gathered("x1", x1, d)
    entered(("wg", 1))
    entered(("wu", 1))
    pre(0, 1)

    def pick1(h):
        each(lambda k: pick(h, x1[k, :, half(h)], xg, k))

    pick1(0)
    for h in range(2):
        each(lambda k: pick_scales(1, h, k))
    entered(("wd", 1))

    def finish(t, h, ds):
        for d in ds:
            put(t, halved(t, h, d), PLACE[d])
            give_mate(t, h, d)

    post_rows(0, 0, 1, 5, 3)
    finish(0, 0, (4, 3, 5))
    for h in range(2):
        far(0, h)
        near(0, h)
    post_rows(0, 0, 1, 3, 2)
    finish(0, 0, (2, 6))
    post_rows(0, 0, 1, 0, 3)
    finish(0, 0, (1, 7, 0))
    step(0, 3, 0, 1)
    pre(0, 0)
    step(0, 2, 1, 0)
    step(0, 3, 2, 3)
    pre(0, 1)
    step(0, 2, 0, 1)
    step(0, 2, 3, 2)
    pick1(1)
    pre(1, 0)
    step(0, 1, 0, 0)
    step(0, 1, 1, 1)
    step(0, 2, 2, 3)
    pre(1, 1)
    step(0, 1, 3, 2)

    def passing(quarter):
        for ch in (2 * quarter, 2 * quarter + 1):
            scatter_last(0, ch, xg0.at[0, 0, 1])
            at = rows(ch, FINE)
            send(("pass", ch), tot.at[0, at], g1.at[0, 0, at], pass_to, "pass")

    def passed(quarter):
        for ch in (2 * quarter, 2 * quarter + 1):
            sent["pass", ch].wait_recv()
            gather_first("g1", g1, ch, FINE)

    passing(0)
    passing(1)
    step(0, 1, 2, 3)
    passed(0)
    passed(1)
    passing(2)
    passing(3)

    def level(d, h, i):
        up, down = 4 * h + 2 * i, 4 * h + 2 - 2 * i
        gather_step("g1", g1, d, ((up, down), (up + 1, down + 1)), FINE)

    def take(h, ds):
        for d in ds:
            gathered("g1", g1, d, h, half(h))
            pick(h, g1[PLACE[d], :, half(h)], gg, PLACE[d])

    level(1, 0, 0)
    level(1, 0, 1)
    take(0, (0,))
    passed(2)
    passed(3)
    level(2, 0, 0)
    level(2, 0, 1)
    take(0, (1, 7))
    level(1, 1, 0)
    level(1, 1, 1)
    take(0, (2, 6))
    post_rows(1, 0, 0, 0, 5)
    level(3, 0, 0)
    level(3, 0, 1)
    post_rows(1, 0, 1, 0, 5)
    level(2, 1, 0)
    take(0, (3, 5))
    post_rows(1, 0, 0, 5, 2)
    level(2, 1, 1)
    post_rows(1, 0, 1, 5, 2)
    level(4, 0, 0)
    finish(1, 0, (3, 5))
    level(3, 1, 0)
    take(0, (4,))
    post_rows(1, 0, 0, 7, 1)
    level(3, 1, 1)
    near(1, 0)
    post_rows(1, 0, 1, 7, 1)
    finish(1, 0, (4, 2, 6))
    level(4, 1, 0)
    far(1, 0)
    finish(1, 0, (1, 7, 0))
    take(1, (4, 3, 5))
    step(1, 2, 1, 0)
    post_rows(1, 1, 0, 5, 3)
    step(1, 3, 0, 1)
    post_rows(1, 1, 1, 5, 3)
    finish(1, 1, (4, 3, 5))
    step(1, 2, 0, 1)
    far(1, 1)
    near(1, 1)
    def final(quarter):
        for ch in (2 * quarter, 2 * quarter + 1):
            scatter_last(1, ch, g1.at[0, 0])
        at = rows(quarter, 4)
        enter(("fin", quarter), [(tot.at[1, at], out_ref.at[at])], out_ref.at[at])

    take(1, (2, 6))
    post_rows(1, 1, 0, 3, 2)
    post_rows(1, 1, 1, 3, 2)
    finish(1, 1, (2, 6))
    step(1, 1, 0, 0)
    step(1, 3, 2, 3)
    take(1, (0, 1, 7))
    step(1, 2, 3, 2)
    post_rows(1, 1, 0, 0, 3)
    step(1, 1, 1, 1)
    post_rows(1, 1, 1, 0, 3)
    step(1, 2, 2, 3)
    finish(1, 1, (1, 7, 0))
    final(0)
    step(1, 1, 3, 2)
    final(1)
    step(1, 1, 2, 3)
    final(2)
    final(3)
    for quarter in range(4):
        entered(("fin", quarter))

    for name, buf in (("a", xg0), ("x1", x1), ("g1", g1), ("t", tab)):
        group = ("t", "c") if name == "t" else (name, "c", 0, 0)
        make((name, "z"), group, buf.at[0:7, 0], buf.at[0:7, 1], z_up).wait_send()
        make((name, "c"), group, buf.at[:, 0], buf.at[:, 1], mate).wait_send()
    for t in range(2):
        make((t, "rz"), (t, "rc", 0, 0), part.at[t, 0:7, 0], part.at[t, 0:7, 0], z_up).wait_send()
        make((t, "rc"), (t, "rc", 0, 0), part.at[t, :, 1], part.at[t, :, 1], mate).wait_send()
    make("pass", ("pass", 0), tot.at[0], tot.at[0], pass_to).wait_send()

    @pl.when(mixed)
    def _():
        for key, whole in ends:
            make(key, key, whole, whole, swap).wait_send()

    assert len(senders) <= SENDERS and len(takers) <= TAKERS, (len(senders), len(takers))

def shards(grad_out, saved_inputs, routes, gate_weights, w_gate, w_up, w_down):
    block = pltpu.VMEM((RING, 2, TOK, D), BF)
    return pl.pallas_call(
        kernel,
        out_shape=jax.ShapeDtypeStruct((TOK, D), BF),
        in_specs=[pl.BlockSpec(memory_space=pl.ANY)] * 7,
        out_specs=pl.BlockSpec(memory_space=pl.ANY),
        scratch_shapes=[
            pltpu.VMEM((RING, 2, 2, TOK, D), BF),
            block, block,
            pltpu.VMEM((RING, 2, 2, 16, TOK), F32),
            pltpu.VMEM((2, D, H), BF),
            pltpu.VMEM((2, D, H), BF),
            pltpu.VMEM((2, H, D), BF),
            pltpu.VMEM((2, RING, 2, TOK, D), BF),
            pltpu.VMEM((2, RING, TOK, D), BF),
            pltpu.VMEM((2, 4, TOK, D), BF),
            pltpu.VMEM((2, 4, TOK, D), BF),
            pltpu.VMEM((2, TOK, D), BF),
            pltpu.VMEM((2, RING * CAP, D), BF),
            pltpu.VMEM((2, RING * CAP, D), BF),
            pltpu.VMEM((2, 2, RING * CAP, H), F32),
            pltpu.VMEM((2, 2, RING * CAP, H), F32),
            pltpu.VMEM((RING, 2 * CAP, D), BF),
            pltpu.VMEM((3, 2, RING * CAP, 1), F32),
            pltpu.VMEM((16, 256), F32),
            pltpu.VMEM((RING, 256, 2), F32),
            pltpu.VMEM((2, 16, 128), F32),
            pltpu.VMEM((2, RING, 128, 2), F32),
            pltpu.VMEM((2, 8, TOK), jnp.int32),
            pltpu.VMEM((2, 16, TOK), F32),
            pltpu.SemaphoreType.DMA((SENDERS,)),
            pltpu.SemaphoreType.DMA((TAKERS,)),
            pltpu.SemaphoreType.DMA((20,)),
        ],
        compiler_params=pltpu.CompilerParams(
            collective_id=0, has_side_effects=True, vmem_limit_bytes=63 << 20
        ),
        name="moe_back",
    )(
        grad_out[0],
        saved_inputs[0],
        jnp.swapaxes(routes[0], 1, 2),
        jnp.swapaxes(gate_weights[0], 1, 2),
        w_gate[0],
        w_up[0],
        w_down[0],
    )[None]


def solution(mesh):
    placed = (
        P("section", "expert", None),
        P("section", None, "expert", None),
        P("section", None, "expert", None),
        P("section", None, "expert", None),
        P("section", "expert", None, None),
        P("section", "expert", None, None),
        P("section", "expert", None, None),
    )
    return jax.shard_map(
        shards, mesh=mesh, in_specs=placed, out_specs=P("section", "expert", None), check_vma=False
    )
```

time: 171 us -> 168 us (0.982)
  Pallas kernels: 170 us -> 166 us
    pallas_call x1, Pallas kernels: 170 us -> 166 us  [shards(): pl.pallas_call(kernel, out_shape=jax.ShapeDtypeStruct((TOK, D), BF), in_s...]
where the time goes in v3:
time: 168 us
  Pallas kernels  166 us (99%)
    pallas_call x1, Pallas kernels, shards(): pl.pallas_call(kernel, out_shape=jax.ShapeDtypeStruct((TOK, D), BF), in_s...  166 us

profile of v3, /device:TPU:1, one launch (start us, length us, event | category | flops | bytes accessed | tf_op | source)
XLA Modules:
  0.0 167.7 jit_solution(18294500298815321243)
XLA Ops:
  0.0 166.1 %moe_back.1 = bf16[128,1024]{1,0:T(8,128)(2,1)} custom-call(bf16[128,1024]{1,0:T(8,128)(2,1)} %bitcast.17, bf16[2,128,1024]{2,1,0:T(8,128)(2,1)} %bitcast.16, s32[2,8,128]{2,1,0:T(8,128)} %bitcast.18, f32[2,8,128]{2,1,0:T(8,128)} %bitcast.19, bf16[2,1024,512]{2,1,0:T(8,128)(2,1)} %bitcast.12, bf16[2,1024,512]{2,1,0:T(8,128)(2,1)} %bitcast.13, ...), custom_call_target="tpu_custom_call" | custom-call | tf_op jit(solution)/shard_map/moe_back/pallas_call | solution.py:552
  166.1 1.7 copy.9

commit v4 on v3

--- a/solution.py
+++ b/solution.py
@@ -14,7 +14,7 @@
 RING = 8
 PLACE = {0: 0, 1: 1, 7: 2, 2: 3, 6: 4, 3: 5, 5: 6, 4: 7}
 SENDERS = 40
-TAKERS = 162
+TAKERS = 166
 FINE = 8
 
 
@@ -493,43 +493,44 @@
     finish(1, 0, (4, 2, 6))
     level(4, 1, 0)
     far(1, 0)
-    finish(1, 0, (1, 7, 0))
-    take(1, (4, 3, 5))
+    take(1, (3, 5, 4))
     step(1, 2, 1, 0)
     post_rows(1, 1, 0, 5, 3)
+    post_rows(1, 1, 1, 5, 3)
     step(1, 3, 0, 1)
-    post_rows(1, 1, 1, 5, 3)
     finish(1, 1, (4, 3, 5))
+    finish(1, 0, (1, 7, 0))
+    far(1, 1)
     step(1, 2, 0, 1)
-    far(1, 1)
     near(1, 1)
+
     def final(quarter):
         for ch in (2 * quarter, 2 * quarter + 1):
             scatter_last(1, ch, g1.at[0, 0])
-        at = rows(quarter, 4)
-        enter(("fin", quarter), [(tot.at[1, at], out_ref.at[at])], out_ref.at[at])
+            at = rows(ch, FINE)
+            enter(("fin", ch), [(tot.at[1, at], out_ref.at[at])], out_ref.at[at])
 
     take(1, (2, 6))
     post_rows(1, 1, 0, 3, 2)
     post_rows(1, 1, 1, 3, 2)
     finish(1, 1, (2, 6))
+    step(1, 3, 2, 3)
     step(1, 1, 0, 0)
-    step(1, 3, 2, 3)
     take(1, (0, 1, 7))
     step(1, 2, 3, 2)
     post_rows(1, 1, 0, 0, 3)
+    step(1, 2, 2, 3)
     step(1, 1, 1, 1)
     post_rows(1, 1, 1, 0, 3)
-    step(1, 2, 2, 3)
     finish(1, 1, (1, 7, 0))
     final(0)
-    step(1, 1, 3, 2)
+    step(1, 1, 2, 2)
     final(1)
-    step(1, 1, 2, 3)
+    step(1, 1, 3, 3)
     final(2)
     final(3)
-    for quarter in range(4):
-        entered(("fin", quarter))
+    for ch in range(FINE):
+        entered(("fin", ch))
 
     for name, buf in (("a", xg0), ("x1", x1), ("g1", g1), ("t", tab)):
         group = ("t", "c") if name == "t" else (name, "c", 0, 0)

time: 168 us -> 168 us (level)
  no operation moved by 1% of the time
where the time goes in v4:
time: 168 us
  Pallas kernels  166 us (99%)
    pallas_call x1, Pallas kernels, shards(): pl.pallas_call(kernel, out_shape=jax.ShapeDtypeStruct((TOK, D), BF), in_s...  166 us

profile of v4, /device:TPU:1, one launch (start us, length us, event | category | flops | bytes accessed | tf_op | source)
XLA Modules:
  0.0 167.7 jit_solution(370125646166145485)
XLA Ops:
  0.0 166.0 %moe_back.1 = bf16[128,1024]{1,0:T(8,128)(2,1)} custom-call(bf16[128,1024]{1,0:T(8,128)(2,1)} %bitcast.17, bf16[2,128,1024]{2,1,0:T(8,128)(2,1)} %bitcast.16, s32[2,8,128]{2,1,0:T(8,128)} %bitcast.18, f32[2,8,128]{2,1,0:T(8,128)} %bitcast.19, bf16[2,1024,512]{2,1,0:T(8,128)(2,1)} %bitcast.12, bf16[2,1024,512]{2,1,0:T(8,128)(2,1)} %bitcast.13, ...), custom_call_target="tpu_custom_call" | custom-call | tf_op jit(solution)/shard_map/moe_back/pallas_call | solution.py:553
  166.0 1.7 copy.9

commit v5 on v4

--- a/solution.py
+++ b/solution.py
@@ -35,15 +35,15 @@
     e = lax.axis_index("expert")
     core = lax.rem(s, 2)
     x_lo = lax.rem(e, 2)
-    mixed = core != x_lo
+    mixed = core == x_lo
     other_core = s + 1 - 2 * core
     other_x = e + 1 - 2 * x_lo
     z_up = (s, lax.rem(e + 2, 16))
     z_down = (s, lax.rem(e + 14, 16))
     mate = (other_core, e)
     swap = (other_core, other_x)
-    pass_to = (lax.rem(s + 16 - 2 * (1 - x_lo), 16), other_x)
-    pass_from = (lax.rem(s + 2 * x_lo, 16), other_x)
+    pass_to = (lax.rem(s + 16 - 2 * x_lo, 16), other_x)
+    pass_from = (lax.rem(s + 2 * (1 - x_lo), 16), other_x)
     home = lax.select(mixed, other_x, e)
 
     barrier = pltpu.get_barrier_semaphore()

time: 168 us -> 166 us (0.988); the launches traced: 168 us -> 164 us
  Pallas kernels: 166 us -> 162 us
    pallas_call x1, Pallas kernels: 166 us -> 162 us  [shards(): pl.pallas_call(kernel, out_shape=jax.ShapeDtypeStruct((TOK, D), BF), in_s...]
where the time goes in v5:
time: 166 us; the launch traced here: 164 us
  Pallas kernels  162 us (98%)
  local copies, waits for them, and re-layouts  1.67 us (1%)
    pallas_call x1, Pallas kernels, shards(): pl.pallas_call(kernel, out_shape=jax.ShapeDtypeStruct((TOK, D), BF), in_s...  162 us

profile of v5, /device:TPU:1, one launch (start us, length us, event | category | flops | bytes accessed | tf_op | source)
XLA Modules:
  0.0 163.5 jit_solution(12070106333260827888)
XLA Ops:
  0.0 161.8 %moe_back.1 = bf16[128,1024]{1,0:T(8,128)(2,1)} custom-call(bf16[128,1024]{1,0:T(8,128)(2,1)} %bitcast.17, bf16[2,128,1024]{2,1,0:T(8,128)(2,1)} %bitcast.16, s32[2,8,128]{2,1,0:T(8,128)} %bitcast.18, f32[2,8,128]{2,1,0:T(8,128)} %bitcast.19, bf16[2,1024,512]{2,1,0:T(8,128)(2,1)} %bitcast.12, bf16[2,1024,512]{2,1,0:T(8,128)(2,1)} %bitcast.13, ...), custom_call_target="tpu_custom_call" | custom-call | tf_op jit(solution)/shard_map/moe_back/pallas_call | solution.py:553
  161.9 1.7 %copy.9 = bf16[1,128,1024]{2,1,0:T(8,128)(2,1)} copy(bf16[1,128,1024]{2,1,0:T(8,128)(2,1)} %bitcast.15) | data formatting | bytes 524288

commit v6 on v5

--- a/solution.py
+++ b/solution.py
@@ -13,8 +13,8 @@
 CAP = 80
 RING = 8
 PLACE = {0: 0, 1: 1, 7: 2, 2: 3, 6: 4, 3: 5, 5: 6, 4: 7}
-SENDERS = 40
-TAKERS = 166
+SENDERS = 31
+TAKERS = 152
 FINE = 8
 
 
@@ -58,6 +58,8 @@
     def make(batch, group, src, dst, peer):
         if group[0] == 1:
             group = (0,) + group[1:]
+        elif group[0] == "x1" and group[1:2] != ("c",) and len(group) == 4:
+            group = ("a",) + group[1:]
         elif group[0] == "g1" and group[1] == "c":
             group = ("a",) + group[1:]
         elif group[0] == "g1":
@@ -519,9 +521,9 @@
     take(1, (0, 1, 7))
     step(1, 2, 3, 2)
     post_rows(1, 1, 0, 0, 3)
+    post_rows(1, 1, 1, 0, 3)
     step(1, 2, 2, 3)
     step(1, 1, 1, 1)
-    post_rows(1, 1, 1, 0, 3)
     finish(1, 1, (1, 7, 0))
     final(0)
     step(1, 1, 2, 2)

time: 166 us -> 166 us (level)
  no operation moved by 1% of the time
where the time goes in v6:
time: 166 us; the launch traced here: 164 us
  Pallas kernels  162 us (98%)
  local copies, waits for them, and re-layouts  1.67 us (1%)
    pallas_call x1, Pallas kernels, shards(): pl.pallas_call(kernel, out_shape=jax.ShapeDtypeStruct((TOK, D), BF), in_s...  162 us

profile of v6, /device:TPU:1, one launch (start us, length us, event | category | flops | bytes accessed | tf_op | source)
XLA Modules:
  0.0 163.8 jit_solution(17819130921917035074)
XLA Ops:
  0.0 162.1 %moe_back.1 = bf16[128,1024]{1,0:T(8,128)(2,1)} custom-call(bf16[128,1024]{1,0:T(8,128)(2,1)} %bitcast.17, bf16[2,128,1024]{2,1,0:T(8,128)(2,1)} %bitcast.16, s32[2,8,128]{2,1,0:T(8,128)} %bitcast.18, f32[2,8,128]{2,1,0:T(8,128)} %bitcast.19, bf16[2,1024,512]{2,1,0:T(8,128)(2,1)} %bitcast.12, bf16[2,1024,512]{2,1,0:T(8,128)(2,1)} %bitcast.13, ...), custom_call_target="tpu_custom_call" | custom-call | tf_op jit(solution)/shard_map/moe_back/pallas_call | solution.py:555
  162.1 1.7 %copy.9 = bf16[1,128,1024]{2,1,0:T(8,128)(2,1)} copy(bf16[1,128,1024]{2,1,0:T(8,128)(2,1)} %bitcast.15) | data formatting | bytes 524288
